TPU v7x, 512 devices: a whole 4x4x16 slice. The times are simulated.
512 devices in a mesh: section: 4 (over x), trial: 128 (over z, y, core).
Axes of the slice: x: 4, y: 4, z: 16, core: 2. Of those that a mesh axis runs over, the one named last changes fastest.
Arguments:
- spike_rates: bfloat16 [512, 256, 256], P(None, 'trial'), may hold values from -6 to 6
- first_preactivation: bfloat16 [1024, 256, 256], P('section', 'trial'), may hold values from -6 to 6
- second_preactivation: bfloat16 [1024, 256, 256], P('section', 'trial'), may hold values from -6 to 6
- output_gradient: bfloat16 [1024, 256, 256], P('section', 'trial'), may hold values from -0.29882812 to 0.29882812
- first_kernel: bfloat16 [3, 1024, 1024], P(None, None, 'section'), may hold values from -0.109375 to 0.109375
- second_kernel: bfloat16 [3, 1024, 1024], P(None, None, 'section'), may hold values from -0.109375 to 0.109375
- session_of: int32 [256], P('trial'), may hold values from 0 to 127, never falling along the last dimension, each value on 1 to 6 neighbouring positions
Outputs:
- readin_grad: bfloat16 [128, 512, 1024], P(None, 'trial', 'section')
Inputs may be any that keep to these rules, and one draw needn't show every extreme that they name: `session_of`: the trials of a session are consecutive; every session has 1 to 6 trials, and one has exactly 6.
All inputs are finite; a program needn't handle non-finite values.
Results may differ from a plain program's by a relative error of at most 0.017.
Values may be sent and summed in bfloat16 or wider, within the bound.
No kernel may reach another device: no remote copies, remote signals or barrier semaphores. Data moves between devices by JAX's collectives and lax.ppermute only.
A program may use at most 64 MiB of HBM per device.

v0:
```python
import math

import jax
import jax.numpy as jnp
from jax import lax
from jax.sharding import PartitionSpec as P

FIRST_DILATION = 32
SECOND_DILATION = 64
MOST = 6


def gelu_slope(preact):
    values = preact.astype(jnp.float32)
    normal_cdf = 0.5 * (1.0 + lax.erf(values * (1.0 / math.sqrt(2.0))))
    density = jnp.exp(-0.5 * values * values) * (1.0 / math.sqrt(2.0 * math.pi))
    return normal_cdf + values * density


def shift_ahead(values, offset):
    padding = [(0, 0)] * (values.ndim - 1) + [(0, offset)]
    return jnp.pad(values[..., offset:], padding)


def tap_sum(weights, flow_grad, spacing):
    running = None
    for kernel_tap in range(3):
        term_tap = lax.dot_general(
            weights[kernel_tap],
            flow_grad,
            (((1,), (0,)), ((), ())),
            preferred_element_type=jnp.float32,
        )
        if kernel_tap > 0:
            term_tap = shift_ahead(term_tap, kernel_tap * spacing)
        running = term_tap if running is None else running + term_tap
    return running


def layer_backprop(upstream, preact, turned, spacing):
    flow_grad = (upstream.astype(jnp.float32) * gelu_slope(preact)).astype(jnp.bfloat16)
    back_sum = tap_sum(turned, lax.all_gather(flow_grad, "section", axis=0, tiled=True), spacing)
    return (upstream.astype(jnp.float32) + back_sum).astype(jnp.bfloat16)


def body(
    spike_rates,
    first_preactivation,
    second_preactivation,
    output_gradient,
    first_kernel,
    second_kernel,
    session_of,
):
    first_flipped_kernel, second_flipped_kernel = (
        lax.all_to_all(first_kernel, "section", split_axis=1, concat_axis=2, tiled=True),
        lax.all_to_all(second_kernel, "section", split_axis=1, concat_axis=2, tiled=True),
    )
    upstream_gradient = layer_backprop(
        output_gradient, second_preactivation, second_flipped_kernel, SECOND_DILATION
    )
    input_gradient = layer_backprop(
        upstream_gradient, first_preactivation, first_flipped_kernel, FIRST_DILATION
    )
    trial_shards = lax.axis_size("trial")
    neurons, trials, steps_count = spike_rates.shape
    neuron_blocks = spike_rates.reshape(trial_shards, neurons // trial_shards, trials, steps_count)
    partials = jnp.einsum(
        "jbil,cil->jibc", neuron_blocks, input_gradient, preferred_element_type=jnp.float32
    )
    arrived = lax.all_to_all(
        partials.astype(jnp.bfloat16), "trial", split_axis=0, concat_axis=0, tiled=True
    ).astype(partials.dtype)
    every_id = lax.all_gather(session_of, "trial", axis=0, tiled=True)
    total_trials = every_id.shape[0]
    flat_parts = arrived.reshape(total_trials, -1)
    session_list = jnp.arange(trial_shards, dtype=jnp.int32)
    first_trial = jnp.sum((every_id[None, :] < session_list[:, None]).astype(jnp.int32), axis=1)

    def add_offset(offset, running):
        position = first_trial + offset
        clipped = jnp.minimum(position, total_trials - 1)
        rows_here = jnp.take(flat_parts, clipped, axis=0)
        valid = (position < total_trials) & (jnp.take(every_id, clipped, axis=0) == session_list)
        return running + jnp.where(valid[:, None], rows_here, 0.0)

    start_sums = jnp.zeros((trial_shards, flat_parts.shape[1]), jnp.float32)
    summed = lax.fori_loop(0, MOST, add_offset, start_sums)
    return summed.reshape(trial_shards, neurons // trial_shards, input_gradient.shape[0]).astype(
        jnp.bfloat16
    )


def solution(mesh):
    in_specs = (
        P(None, "trial", None),
        P("section", "trial", None),
        P("section", "trial", None),
        P("section", "trial", None),
        P(None, None, "section"),
        P(None, None, "section"),
        P("trial"),
    )
    out_specs = P(None, "trial", "section")
    return jax.shard_map(body, mesh=mesh, in_specs=in_specs, out_specs=out_specs, check_vma=False)
```

profile of v0, /device:TPU:1, one launch (start us, length us, event | category | flops | bytes accessed | tf_op | source)
XLA Modules:
  0.0 184.7 jit_solution(364001516441620479)
XLA Ops:
  6.5 1.2 copy.50
  9.9 2.7 %copy.52 = bf16[3,1024,256]{2,0,1:T(4,128)(2,1)} copy(bf16[3,1024,256]{2,1,0:T(8,128)(2,1)S(1)} %copy-done.3) | data formatting | bytes 3145728 | tf_op args[5]
  12.6 5.0 %all-to-all-start = ((bf16[3,1024,256]{2,0,1:T(4,128)(2,1)}), bf16[3,1024,256]{2,0,1:T(4,128)(2,1)S(1)}, u32[]{:S(2)}, u32[]{:S(2)}) async-start(bf16[3,1024,256]{2,0,1:T(4,128)(2,1)} %copy.52), calls=%async_computation | async-start | bytes 4194304 | tf_op jit(solution)/shard_map/all_to_all | solution.py:57
  17.7 21.5 %all-to-all-done = bf16[3,1024,256]{2,0,1:T(4,128)(2,1)S(1)} async-done(((bf16[3,1024,256]{2,0,1:T(4,128)(2,1)}), bf16[3,1024,256]{2,0,1:T(4,128)(2,1)S(1)}, u32[]{:S(2)}, u32[]{:S(2)}) %all-to-all-start) | async-done | bytes 1572896 | tf_op jit(solution)/shard_map/all_to_all | solution.py:57
  39.2 1.5 copy.79
  42.4 14.1 %all-gather.3.cloned.1.call-done = bf16[1024,2,256]{0,2,1:T(8,128)(2,1)} async-done(((bf16[256,2,256]{0,2,1:T(8,128)(2,1)}), bf16[1024,2,256]{0,2,1:T(8,128)(2,1)}) %all-gather.3.cloned.1.call-update) | async-done | bytes 1048592 | tf_op jit(solution)/shard_map/all_gather | solution.py:42
  56.5 1.8 convolution_bitcast_fusion.4
  58.8 1.5 fusion.31
  60.3 1.4 copy.55
  61.7 30.1 %all_to_all.35 = bf16[3,1024,256]{2,0,1:T(4,128)(2,1)S(1)} all-to-all(bf16[3,1024,256]{2,0,1:T(4,128)(2,1)S(1)} %copy.55), channel_id=1, replica_groups=mesh['section'=4,'trial'=128] {'section'}, dimensions={1} | all-to-all | bytes 3145728 | tf_op jit(solution)/shard_map/all_to_all | solution.py:56
  92.7 8.3 %all-gather.5.cloned.1.call-done = bf16[1024,2,256]{0,2,1:T(8,128)(2,1)} async-done(((bf16[256,2,256]{0,2,1:T(8,128)(2,1)}), bf16[1024,2,256]{0,2,1:T(8,128)(2,1)}) %all-gather.5.cloned.1.call-update) | async-done | bytes 1048592 | tf_op jit(solution)/shard_map/all_gather | solution.py:42
  101.1 1.8 convolution_bitcast_fusion.1
  103.4 2.0 %fusion.3 = bf16[128,2,4,256]{0,3,2,1:T(8,128)(2,1)S(1)} fusion(f32[256,2,256]{0,2,1:T(8,128)} %get-tuple-element.154, bf16[1024,2,256]{0,2,1:T(8,128)(2,1)S(1)} %copy-done.1, bf16[256,1024,1]{0,1,2:T(8,128)(2,1)S(1)} %bitcast.90, bf16[128,4,2,256]{3,2,1,0:T(2,128)(2,1)S(1)} %bitcast.84, f32[256,2,192]{0,2,1:T(8,128)S(1)} %slice.59, ...), kind=kOutput, calls=%fused_computation.13 | convolution fusion | flops 403439616 | bytes 3997696 | tf_op jit(solution)/shard_map/jbil,cil->jibc/dot_general | solution.py:68
  105.4 1.2 copy.65
  106.6 19.5 %all-to-all-start.2 = ((bf16[128,2,4,256]{3,2,1,0:T(4,128)(2,1)}), bf16[128,2,4,256]{3,2,1,0:T(4,128)(2,1)S(1)}, u32[]{:S(2)}, u32[]{:S(2)}) async-start(bf16[128,2,4,256]{3,2,1,0:T(4,128)(2,1)} %copy.65), calls=%async_computation.2 | async-start | bytes 1048576 | tf_op jit(solution)/shard_map/all_to_all | solution.py:71
  126.1 1.2 dynamic-slice
  128.1 34.7 %all-reduce.4 = s32[256]{0:T(256)S(1)} all-reduce(s32[256]{0:T(256)S(1)} %dynamic-update-slice), channel_id=1, replica_groups=mesh['section'=4,'trial'=128] {'trial'}, use_global_device_ids=true, to_apply=%add.4 | all-reduce | flops 256 | bytes 2048
  163.1 13.8 %while.14 = (s32[]{:T(128)}, f32[128,1024]{1,0:T(8,128)S(1)}, s32[128]{0:T(128)S(1)}, s32[256]{0:T(256)S(1)}, f32[256,1024]{1,0:T(8,128)S(1)}, /*index=5*/s32[]{:T(128)}, s32[]{:T(128)}) while((s32[]{:T(128)}, f32[128,1024]{1,0:T(8,128)S(1)}, s32[128]{0:T(128)S(1)}, s32[256]{0:T(256)S(1)}, f32[256,1024]{1,0:T(8,128)S(1)}, ...), condition=%wide.region_2.3_spmd.clone, body=%wide.region_1.2_spmd.clone.sunk | while | flops 527491 | bytes 2630751 | solution.py:88
  163.2 1.3 gather_fusion.1
  165.4 1.3 gather_fusion.1
  167.7 1.3 gather_fusion.1
  170.0 1.3 gather_fusion.1
  172.3 1.3 gather_fusion.1
  174.6 1.3 gather_fusion.1
  (74 shorter events, 13.1 us)
Async XLA Ops:
  6.5 96.8 %copy-start = (bf16[512,2,256]{2,1,0:T(2,128)(2,1)S(1)}, bf16[512,2,256]{2,1,0:T(2,128)(2,1)}, u32[]{:S(2)}) copy-start(bf16[512,2,256]{2,1,0:T(2,128)(2,1)} %param.9) | copy-start | bytes 1572868
  6.5 3.4 %copy-start.3 = (bf16[3,1024,256]{2,1,0:T(8,128)(2,1)S(1)}, bf16[3,1024,256]{2,1,0:T(8,128)(2,1)}, u32[]{:S(2)}) copy-start(bf16[3,1024,256]{2,1,0:T(8,128)(2,1)} %param.14) | copy-start | bytes 4718596
  6.5 49.9 %all-gather.3.cloned.1.call-start = ((), (), s32[]{:S(2)}) async-start(), calls=%async_computation.3 | async-start | bytes 1310720 | tf_op jit(solution)/shard_map/all_gather | solution.py:42
  12.6 5.0 %copy-start.5 = (bf16[256,2,256]{2,1,0:T(2,128)(2,1)S(1)}, bf16[256,2,256]{2,1,0:T(2,128)(2,1)}, u32[]{:S(2)}) copy-start(bf16[256,2,256]{2,1,0:T(2,128)(2,1)} %param.10) | copy-start | bytes 786436
  12.6 26.7 %all-to-all-start = ((bf16[3,1024,256]{2,0,1:T(4,128)(2,1)}), bf16[3,1024,256]{2,0,1:T(4,128)(2,1)S(1)}, u32[]{:S(2)}, u32[]{:S(2)}) async-start(bf16[3,1024,256]{2,0,1:T(4,128)(2,1)} %copy.52), calls=%async_computation | async-start | bytes 4194304 | tf_op jit(solution)/shard_map/all_to_all | solution.py:57
  17.6 83.5 %all-gather.5.cloned.1.call-start = ((), (), s32[]{:S(2)}) async-start(), calls=%async_computation.4 | async-start | bytes 1310720 | tf_op jit(solution)/shard_map/all_gather | solution.py:42
  56.5 1.8 copy-start.2
  58.8 1.5 copy-start.4
  101.1 1.8 copy-start.1
  105.4 22.5 %copy-start.6 = (s32[2]{0:T(128)S(1)}, s32[2]{0:T(128)}, u32[]{:S(2)}) copy-start(s32[2]{0:T(128)} %param.15) | copy-start | bytes 28
  106.6 56.4 %all-to-all-start.2 = ((bf16[128,2,4,256]{3,2,1,0:T(4,128)(2,1)}), bf16[128,2,4,256]{3,2,1,0:T(4,128)(2,1)S(1)}, u32[]{:S(2)}, u32[]{:S(2)}) async-start(bf16[128,2,4,256]{3,2,1,0:T(4,128)(2,1)} %copy.65), calls=%async_computation.2 | async-start | bytes 1048576 | tf_op jit(solution)/shard_map/all_to_all | solution.py:71
Sparse Core Ops, SparseCore 0:
  10.0 46.4 all-gather.2
  60.4 40.5 all-gather.4
where the time goes:
time: 187 us; the launch traced here: 185 us
  blocking collectives  64.8 us (35%)
  waiting for transfers between devices  44 us (24%)
  local copies, waits for them, and re-layouts  26.8 us (14%)
  starting transfers between devices  24.5 us (13%)
  between operations  14.2 us (8%)
  matrix products  7.88 us (4%)
  other arithmetic  2.14 us (1%)
    unnamed x1, blocking collectives  34.7 us
    all_to_all x1, blocking collectives, body(): lax.all_to_all(first_kernel, 'section', split_axis=1, concat_axis=2, tile...  30.1 us
    all_gather x2, waiting for transfers between devices, layer_backprop(): lax.all_gather(flow_grad, 'section', axis=0, tiled=True)  22.4 us
    all_to_all x1, waiting for transfers between devices, body(): lax.all_to_all(second_kernel, 'section', split_axis=1, concat_axis=2, til...  21.5 us
    all_to_all x1, starting transfers between devices, body(): lax.all_to_all(partials.astype(jnp.bfloat16), 'trial', split_axis=0, conc...  19.5 us
    unnamed x23, local copies, waits for them, and re-layouts  8.19 us
    gather x6, local copies, waits for them, and re-layouts, add_offset(): jnp.take(every_id, clipped, axis=0) == session_list  7.59 us
    dot_general x5, matrix products, tap_sum(): lax.dot_general(weights[kernel_tap], flow_grad, (((1,), (0,)), ((), ())),...  5.91 us
  transfers between devices with their start and end apart: 4, of which 3 were waited for; matrix products, arithmetic and copies ran while one was open for 5% of the time, Pallas kernels for 0%

commit v1 on v0

v1 whole, which is shorter than its diff:
```python
import math

import jax
import jax.numpy as jnp
from jax import lax
from jax.sharding import PartitionSpec as P

FIRST_DILATION = 32
SECOND_DILATION = 64


def gelu_slope(preact):
    values = preact.astype(jnp.float32)
    normal_cdf = 0.5 * (1.0 + lax.erf(values * (1.0 / math.sqrt(2.0))))
    density = jnp.exp(-0.5 * values * values) * (1.0 / math.sqrt(2.0 * math.pi))
    return normal_cdf + values * density


def shift_ahead(values, offset):
    padding = [(0, 0)] * (values.ndim - 1) + [(0, offset)]
    return jnp.pad(values[..., offset:], padding)


def layer_backprop(upstream, preact, weights, spacing):
    trials, own, steps = upstream.shape
    flow = (upstream.astype(jnp.float32) * gelu_slope(preact)).astype(jnp.bfloat16)
    stacked = jnp.concatenate([flow] + [shift_ahead(flow, tap * spacing) for tap in (1, 2)], axis=1)
    wide = jnp.concatenate([weights[tap] for tap in range(3)], axis=1)
    partial = jnp.einsum("co,iot->cit", wide, stacked, preferred_element_type=jnp.float32)
    shards = lax.axis_size("section")
    partial = partial.astype(jnp.bfloat16).reshape(shards, own, trials, steps)
    arrived = lax.all_to_all(partial, "section", split_axis=0, concat_axis=0, tiled=True)
    back = jnp.sum(arrived.astype(jnp.float32), axis=0)
    return (upstream.astype(jnp.float32) + back.transpose(1, 0, 2)).astype(jnp.bfloat16)


def body(
    spike_rates,
    first_preactivation,
    second_preactivation,
    output_gradient,
    first_kernel,
    second_kernel,
    session_of,
):
    by_trial = lambda a: a.transpose(1, 0, 2)
    upper = layer_backprop(
        by_trial(output_gradient), by_trial(second_preactivation), second_kernel, SECOND_DILATION
    )
    input_gradient = layer_backprop(upper, by_trial(first_preactivation), first_kernel, FIRST_DILATION)
    shards = lax.axis_size("trial")
    neurons, trials, steps = spike_rates.shape
    own = input_gradient.shape[1]
    block = neurons // shards
    parts = jnp.einsum("nit,ict->nic", spike_rates, input_gradient, preferred_element_type=jnp.float32)
    parts = parts.astype(jnp.bfloat16).reshape(shards, block * trials, own)
    marks = jnp.broadcast_to(session_of.astype(jnp.bfloat16)[None, :, None], (shards, trials, own))
    arrived = lax.all_to_all(
        jnp.concatenate([parts, marks], axis=1), "trial", split_axis=0, concat_axis=0, tiled=True
    )
    ids = arrived[:, block * trials :, 0].astype(jnp.int32).reshape(1, -1)
    rows = arrived[:, : block * trials].reshape(shards, block, trials, own)
    sessions = lax.broadcasted_iota(jnp.int32, (shards, 1), 0)
    chosen = (ids == sessions).astype(jnp.bfloat16).reshape(shards, shards, trials)
    return jnp.einsum("sdi,dnic->snc", chosen, rows, preferred_element_type=jnp.float32).astype(
        jnp.bfloat16
    )


def solution(mesh):
    in_specs = (
        P(None, "trial", None),
        P("section", "trial", None),
        P("section", "trial", None),
        P("section", "trial", None),
        P(None, None, "section"),
        P(None, None, "section"),
        P("trial"),
    )
    out_specs = P(None, "trial", "section")
    return jax.shard_map(body, mesh=mesh, in_specs=in_specs, out_specs=out_specs, check_vma=False)
```

time: 187 us -> 124 us (0.66)
  the two profiles are of different devices: /device:TPU:1 before, /device:TPU:33 now
where the time goes in v1:
time: 124 us
  blocking collectives  77 us (62%)
  waiting for transfers between devices  25 us (20%)
  local copies, waits for them, and re-layouts  9.44 us (8%)
  starting transfers between devices  7.66 us (6%)
  matrix products  2.55 us (2%)
  other arithmetic  2.18 us (2%)
    all_to_all x1, blocking collectives, body(): lax.all_to_all(jnp.concatenate([parts, marks], axis=1), 'trial', split_ax...  77 us
    all_to_all x2, waiting for transfers between devices, layer_backprop(): lax.all_to_all(partial, 'section', split_axis=0, concat_axis=0, tiled=True)  25 us
    all_to_all x2, starting transfers between devices, layer_backprop(): lax.all_to_all(partial, 'section', split_axis=0, concat_axis=0, tiled=True)  7.66 us
    squeeze x2, local copies, waits for them, and re-layouts, layer_backprop(): wide = jnp.concatenate([weights[tap] for tap in range(3)], axis=1)  3.73 us
  transfers between devices with their start and end apart: 2, of which 2 were waited for; matrix products, arithmetic and copies ran while one was open for 2% of the time, Pallas kernels for 0%

profile of v1, /device:TPU:33, one launch (start us, length us, event | category | flops | bytes accessed | tf_op | source)
XLA Modules:
  0.0 124.1 jit_solution(14867937157828472716)
XLA Ops:
  0.0 1.3 %fusion.44 = bf16[2,256,256]{2,1,0:T(8,128)(2,1)S(1)} fusion(bf16[256,2,256]{2,1,0:T(2,128)(2,1)} %param.9, bf16[256,2,256]{2,1,0:T(2,128)(2,1)} %param.10), kind=kLoop, calls=%fused_computation.54 | loop fusion | flops 1572864 | bytes 786432 | tf_op jit(solution)/shard_map/convert_element_type | solution.py:26
  1.3 0.1 slice.48
  1.5 1.5 %slice_bitcast_fusion.5 = (bf16[1024,256]{1,0:T(8,128)(2,1)S(1)}, bf16[1024,256]{1,0:T(8,128)(2,1)S(1)}, bf16[1024,256]{1,0:T(8,128)(2,1)S(1)}) fusion(bf16[3,1024,256]{2,1,0:T(8,128)(2,1)} %param.12), kind=kLoop, calls=%fused_computation.75 | loop fusion | bytes 3145728 | tf_op jit(solution)/shard_map/squeeze | solution.py:28
  3.0 1.0 fusion.14
  4.0 1.1 copy.54
  5.0 4.0 %all-to-all-start = ((bf16[4,256,2,256]{3,1,2,0:T(8,128)(2,1)}), bf16[4,256,2,256]{3,1,2,0:T(8,128)(2,1)S(1)}, u32[]{:S(2)}, u32[]{:S(2)}) async-start(bf16[4,256,2,256]{3,1,2,0:T(8,128)(2,1)} %copy.54), calls=%async_computation | async-start | bytes 2097152 | tf_op jit(solution)/shard_map/all_to_all | solution.py:32
  9.0 2.3 %slice_bitcast_fusion.2 = (bf16[1024,256]{1,0:T(8,128)(2,1)S(1)}, bf16[1024,256]{1,0:T(8,128)(2,1)S(1)}, bf16[1024,256]{1,0:T(8,128)(2,1)}) fusion(bf16[3,1024,256]{2,1,0:T(8,128)(2,1)} %param.11), kind=kLoop, calls=%fused_computation.72 | loop fusion | bytes 3145728 | tf_op jit(solution)/shard_map/squeeze | solution.py:28
  11.3 11.9 %all-to-all-done = bf16[4,256,2,256]{3,1,2,0:T(8,128)(2,1)S(1)} async-done(((bf16[4,256,2,256]{3,1,2,0:T(8,128)(2,1)}), bf16[4,256,2,256]{3,1,2,0:T(8,128)(2,1)S(1)}, u32[]{:S(2)}, u32[]{:S(2)}) %all-to-all-start) | async-done | bytes 1048608 | tf_op jit(solution)/shard_map/all_to_all | solution.py:32
  23.2 0.1 convert_reduce_fusion.1
  23.4 0.8 copy-done.3
  24.2 0.3 fusion.37
  24.7 0.5 copy-done.2
  25.2 1.0 fusion.13
  26.2 1.1 copy.56
  27.2 3.6 %all-to-all-start.1 = ((bf16[4,256,2,256]{3,1,2,0:T(8,128)(2,1)}), bf16[4,256,2,256]{3,1,2,0:T(8,128)(2,1)S(1)}, u32[]{:S(2)}, u32[]{:S(2)}) async-start(bf16[4,256,2,256]{3,1,2,0:T(8,128)(2,1)} %copy.56), calls=%async_computation.1 | async-start | bytes 2097152 | tf_op jit(solution)/shard_map/all_to_all | solution.py:32
  31.0 13.1 %all-to-all-done.1 = bf16[4,256,2,256]{3,1,2,0:T(8,128)(2,1)S(1)} async-done(((bf16[4,256,2,256]{3,1,2,0:T(8,128)(2,1)}), bf16[4,256,2,256]{3,1,2,0:T(8,128)(2,1)S(1)}, u32[]{:S(2)}, u32[]{:S(2)}) %all-to-all-start.1) | async-done | bytes 1048608 | tf_op jit(solution)/shard_map/all_to_all | solution.py:32
  44.1 0.1 convert_reduce_fusion
  44.3 0.3 fusion.17
  44.6 0.5 copy.58
  45.1 0.2 reshape.46
  45.3 0.3 pad_maximum_fusion
  45.6 77.0 %all_to_all.15 = bf16[128,10,256]{2,1,0:T(8,128)(2,1)S(1)} all-to-all(bf16[128,10,256]{2,1,0:T(8,128)(2,1)S(1)} %pad_maximum_fusion), channel_id=1, replica_groups=mesh['section'=4,'trial'=128] {'trial'}, dimensions={0} | all-to-all | bytes 1310720 | tf_op jit(solution)/shard_map/all_to_all | solution.py:58
  122.9 0.3 fusion.18
  123.1 0.9 copy.61
  (18 shorter events, 0.7 us)
Async XLA Ops:
  0.0 44.3 %copy-start = (bf16[512,2,256]{2,1,0:T(2,128)(2,1)S(1)}, bf16[512,2,256]{2,1,0:T(2,128)(2,1)}, u32[]{:S(2)}) copy-start(bf16[512,2,256]{2,1,0:T(2,128)(2,1)} %param.7) | copy-start | bytes 1572868
  5.0 18.2 %all-to-all-start = ((bf16[4,256,2,256]{3,1,2,0:T(8,128)(2,1)}), bf16[4,256,2,256]{3,1,2,0:T(8,128)(2,1)S(1)}, u32[]{:S(2)}, u32[]{:S(2)}) async-start(bf16[4,256,2,256]{3,1,2,0:T(8,128)(2,1)} %copy.54), calls=%async_computation | async-start | bytes 2097152 | tf_op jit(solution)/shard_map/all_to_all | solution.py:32
  11.3 12.1 %copy-start.1 = (bf16[256,2,256]{2,1,0:T(2,128)(2,1)S(1)}, bf16[256,2,256]{2,1,0:T(2,128)(2,1)}, u32[]{:S(2)}) copy-start(bf16[256,2,256]{2,1,0:T(2,128)(2,1)} %param.10) | copy-start | bytes 786436
  23.2 1.0 copy-start.3
  24.2 1.0 copy-start.2
  27.2 3.7 %copy-start.4 = (s32[2]{0:T(128)S(1)}, s32[2]{0:T(128)}, u32[]{:S(2)}) copy-start(s32[2]{0:T(128)} %param.13) | copy-start | bytes 28
  27.2 16.9 %all-to-all-start.1 = ((bf16[4,256,2,256]{3,1,2,0:T(8,128)(2,1)}), bf16[4,256,2,256]{3,1,2,0:T(8,128)(2,1)S(1)}, u32[]{:S(2)}, u32[]{:S(2)}) async-start(bf16[4,256,2,256]{3,1,2,0:T(8,128)(2,1)} %copy.56), calls=%async_computation.1 | async-start | bytes 2097152 | tf_op jit(solution)/shard_map/all_to_all | solution.py:32

commit v2 on v1

--- a/solution.py
+++ b/solution.py
@@ -51,20 +51,21 @@
     shards = lax.axis_size("trial")
     neurons, trials, steps = spike_rates.shape
     own = input_gradient.shape[1]
-    block = neurons // shards
+    rows = neurons // shards * own // 128
     parts = jnp.einsum("nit,ict->nic", spike_rates, input_gradient, preferred_element_type=jnp.float32)
-    parts = parts.astype(jnp.bfloat16).reshape(shards, block * trials, own)
-    marks = jnp.broadcast_to(session_of.astype(jnp.bfloat16)[None, :, None], (shards, trials, own))
+    parts = parts.astype(jnp.bfloat16).reshape(neurons, trials, own // 128, 128)
+    parts = parts.transpose(0, 2, 1, 3).reshape(shards, rows, trials, 128)
+    marks = jnp.broadcast_to(session_of.astype(jnp.bfloat16)[None, None, :, None], (shards, 1, trials, 128))
     arrived = lax.all_to_all(
         jnp.concatenate([parts, marks], axis=1), "trial", split_axis=0, concat_axis=0, tiled=True
     )
-    ids = arrived[:, block * trials :, 0].astype(jnp.int32).reshape(1, -1)
-    rows = arrived[:, : block * trials].reshape(shards, block, trials, own)
-    sessions = lax.broadcasted_iota(jnp.int32, (shards, 1), 0)
-    chosen = (ids == sessions).astype(jnp.bfloat16).reshape(shards, shards, trials)
-    return jnp.einsum("sdi,dnic->snc", chosen, rows, preferred_element_type=jnp.float32).astype(
-        jnp.bfloat16
+    ids = arrived[:, rows, :, 0].astype(jnp.int32)
+    sessions = lax.broadcasted_iota(jnp.int32, (shards, 1, 1), 0)
+    chosen = (ids[None] == sessions).astype(jnp.bfloat16)
+    summed = jnp.einsum(
+        "sdi,dmil->sml", chosen, arrived[:, :rows], preferred_element_type=jnp.float32
     )
+    return summed.astype(jnp.bfloat16).reshape(shards, neurons // shards, own)
 
 
 def solution(mesh):

time: 124 us -> 106 us (0.85)
  the two profiles are of different devices: /device:TPU:33 before, /device:TPU:1 now
where the time goes in v2:
time: 106 us; the launch traced here: 104 us
  blocking collectives  63.3 us (60%)
  waiting for transfers between devices  17.1 us (16%)
  local copies, waits for them, and re-layouts  9.16 us (9%)
  starting transfers between devices  8.49 us (8%)
  other arithmetic  3.16 us (3%)
  matrix products  2.64 us (2%)
    all_to_all x1, blocking collectives, body(): lax.all_to_all(jnp.concatenate([parts, marks], axis=1), 'trial', split_ax...  63.3 us
    all_to_all x2, waiting for transfers between devices, layer_backprop(): lax.all_to_all(partial, 'section', split_axis=0, concat_axis=0, tiled=True)  17.1 us
    all_to_all x2, starting transfers between devices, layer_backprop(): lax.all_to_all(partial, 'section', split_axis=0, concat_axis=0, tiled=True)  8.49 us
    squeeze x2, local copies, waits for them, and re-layouts, layer_backprop(): wide = jnp.concatenate([weights[tap] for tap in range(3)], axis=1)  3.77 us
    convert_element_type x2, other arithmetic, layer_backprop(): (upstream.astype(jnp.float32) * gelu_slope(preact)).astype(jnp.bfloat16)  2.6 us
  transfers between devices with their start and end apart: 2, of which 2 were waited for; matrix products, arithmetic and copies ran while one was open for 2% of the time, Pallas kernels for 0%

profile of v2, /device:TPU:1, one launch (start us, length us, event | category | flops | bytes accessed | tf_op | source)
XLA Modules:
  0.0 104.0 jit_solution(12193835580913491303)
XLA Ops:
  0.0 1.3 %fusion.43 = bf16[2,256,256]{2,1,0:T(8,128)(2,1)S(1)} fusion(bf16[256,2,256]{2,1,0:T(2,128)(2,1)} %param.9, bf16[256,2,256]{2,1,0:T(2,128)(2,1)} %param.10), kind=kLoop, calls=%fused_computation.53 | loop fusion | flops 1572864 | bytes 786432 | tf_op jit(solution)/shard_map/convert_element_type | solution.py:26
  1.3 0.1 slice.48
  1.5 1.5 %slice_bitcast_fusion.5 = (bf16[1024,256]{1,0:T(8,128)(2,1)S(1)}, bf16[1024,256]{1,0:T(8,128)(2,1)S(1)}, bf16[1024,256]{1,0:T(8,128)(2,1)S(1)}) fusion(bf16[3,1024,256]{2,1,0:T(8,128)(2,1)} %param.12), kind=kLoop, calls=%fused_computation.75 | loop fusion | bytes 3145728 | tf_op jit(solution)/shard_map/squeeze | solution.py:28
  3.0 1.0 fusion.14
  4.0 1.0 %copy.44 = bf16[4,256,2,256]{3,1,2,0:T(8,128)(2,1)} copy(bf16[4,256,2,256]{3,1,0,2:T(8,128)(2,1)S(1)} %bitcast.87) | data formatting | bytes 2097152 | tf_op jit(solution)/shard_map/reshape | solution.py:31
  5.0 4.8 %all-to-all-start = ((bf16[4,256,2,256]{3,1,2,0:T(8,128)(2,1)}), bf16[4,256,2,256]{3,1,2,0:T(8,128)(2,1)S(1)}, u32[]{:S(2)}, u32[]{:S(2)}) async-start(bf16[4,256,2,256]{3,1,2,0:T(8,128)(2,1)} %copy.44), calls=%async_computation | async-start | bytes 2097152 | tf_op jit(solution)/shard_map/all_to_all | solution.py:32
  9.8 2.3 %slice_bitcast_fusion.2 = (bf16[1024,256]{1,0:T(8,128)(2,1)S(1)}, bf16[1024,256]{1,0:T(8,128)(2,1)S(1)}, bf16[1024,256]{1,0:T(8,128)(2,1)}) fusion(bf16[3,1024,256]{2,1,0:T(8,128)(2,1)} %param.11), kind=kLoop, calls=%fused_computation.72 | loop fusion | bytes 3145728 | tf_op jit(solution)/shard_map/squeeze | solution.py:28
  12.2 7.4 %all-to-all-done = bf16[4,256,2,256]{3,1,2,0:T(8,128)(2,1)S(1)} async-done(((bf16[4,256,2,256]{3,1,2,0:T(8,128)(2,1)}), bf16[4,256,2,256]{3,1,2,0:T(8,128)(2,1)S(1)}, u32[]{:S(2)}, u32[]{:S(2)}) %all-to-all-start) | async-done | bytes 1048608 | tf_op jit(solution)/shard_map/all_to_all | solution.py:32
  19.6 0.1 convert_reduce_fusion.1
  19.8 1.3 %fusion.36 = bf16[2,256,256]{2,1,0:T(8,128)(2,1)S(1)} fusion(bf16[256,2,256]{2,1,0:T(2,128)(2,1)} %param.8, f32[256,2,256]{2,0,1:T(8,128)S(1)} %convert_reduce_fusion.1, bf16[256,2,256]{2,1,0:T(2,128)(2,1)S(1)} %copy-done.1), kind=kLoop, calls=%fused_computation.46 | loop fusion | flops 1966080 | bytes 1310720 | tf_op jit(solution)/shard_map/convert_element_type | solution.py:26
  21.0 0.1 slice.50
  21.3 1.0 fusion.13
  22.3 1.0 %copy.46 = bf16[4,256,2,256]{3,1,2,0:T(8,128)(2,1)} copy(bf16[4,256,2,256]{3,1,0,2:T(8,128)(2,1)S(1)} %bitcast.88) | data formatting | bytes 2097152 | tf_op jit(solution)/shard_map/reshape | solution.py:31
  23.4 3.6 %all-to-all-start.1 = ((bf16[4,256,2,256]{3,1,2,0:T(8,128)(2,1)}), bf16[4,256,2,256]{3,1,2,0:T(8,128)(2,1)S(1)}, u32[]{:S(2)}, u32[]{:S(2)}) async-start(bf16[4,256,2,256]{3,1,2,0:T(8,128)(2,1)} %copy.46), calls=%async_computation.1 | async-start | bytes 2097152 | tf_op jit(solution)/shard_map/all_to_all | solution.py:32
  27.0 9.7 %all-to-all-done.1 = bf16[4,256,2,256]{3,1,2,0:T(8,128)(2,1)S(1)} async-done(((bf16[4,256,2,256]{3,1,2,0:T(8,128)(2,1)}), bf16[4,256,2,256]{3,1,2,0:T(8,128)(2,1)S(1)}, u32[]{:S(2)}, u32[]{:S(2)}) %all-to-all-start.1) | async-done | bytes 1048608 | tf_op jit(solution)/shard_map/all_to_all | solution.py:32
  36.7 0.1 convert_reduce_fusion
  36.9 0.3 convolution_convert_fusion
  37.2 0.4 copy.48
  37.8 0.3 pad_maximum_fusion
  38.1 0.9 copy.49
  39.0 63.3 %all_to_all.15 = bf16[128,9,2,128]{3,2,1,0:T(2,128)(2,1)S(1)} all-to-all(bf16[128,9,2,128]{3,2,1,0:T(2,128)(2,1)S(1)} %copy.49), channel_id=1, replica_groups=mesh['section'=4,'trial'=128] {'trial'}, dimensions={0} | all-to-all | bytes 1179648 | tf_op jit(solution)/shard_map/all_to_all | solution.py:59
  102.4 0.4 slice.53
  102.8 0.3 fusion.17
  103.2 0.9 copy.52
  (15 shorter events, 0.5 us)
Async XLA Ops:
  0.0 36.9 %copy-start = (bf16[512,2,256]{2,1,0:T(2,128)(2,1)S(1)}, bf16[512,2,256]{2,1,0:T(2,128)(2,1)}, u32[]{:S(2)}) copy-start(bf16[512,2,256]{2,1,0:T(2,128)(2,1)} %param.7) | copy-start | bytes 1572868
  5.0 14.6 %all-to-all-start = ((bf16[4,256,2,256]{3,1,2,0:T(8,128)(2,1)}), bf16[4,256,2,256]{3,1,2,0:T(8,128)(2,1)S(1)}, u32[]{:S(2)}, u32[]{:S(2)}) async-start(bf16[4,256,2,256]{3,1,2,0:T(8,128)(2,1)} %copy.44), calls=%async_computation | async-start | bytes 2097152 | tf_op jit(solution)/shard_map/all_to_all | solution.py:32
  9.8 9.9 %copy-start.1 = (bf16[256,2,256]{2,1,0:T(2,128)(2,1)S(1)}, bf16[256,2,256]{2,1,0:T(2,128)(2,1)}, u32[]{:S(2)}) copy-start(bf16[256,2,256]{2,1,0:T(2,128)(2,1)} %param.10) | copy-start | bytes 786436
  19.7 1.6 %copy-start.2 = (bf16[1024,256]{1,0:T(8,128)(2,1)S(1)}, bf16[1024,256]{1,0:T(8,128)(2,1)}, u32[]{:S(2)}) copy-start(bf16[1024,256]{1,0:T(8,128)(2,1)} %get-tuple-element.10) | copy-start | bytes 1572868
  23.4 3.7 %copy-start.3 = (s32[2]{0:T(128)S(1)}, s32[2]{0:T(128)}, u32[]{:S(2)}) copy-start(s32[2]{0:T(128)} %param.13) | copy-start | bytes 28
  23.4 13.4 %all-to-all-start.1 = ((bf16[4,256,2,256]{3,1,2,0:T(8,128)(2,1)}), bf16[4,256,2,256]{3,1,2,0:T(8,128)(2,1)S(1)}, u32[]{:S(2)}, u32[]{:S(2)}) async-start(bf16[4,256,2,256]{3,1,2,0:T(8,128)(2,1)} %copy.46), calls=%async_computation.1 | async-start | bytes 2097152 | tf_op jit(solution)/shard_map/all_to_all | solution.py:32

commit v3 on v1

v3 whole, which is shorter than its diff:
```python
import math

import jax
import jax.numpy as jnp
from jax import lax
from jax.experimental import pallas as pl
from jax.experimental.pallas import tpu as pltpu
from jax.sharding import PartitionSpec as P

FIRST_DILATION = 32
SECOND_DILATION = 64


def gelu_slope(preact):
    values = preact.astype(jnp.float32)
    normal_cdf = 0.5 * (1.0 + lax.erf(values * (1.0 / math.sqrt(2.0))))
    density = jnp.exp(-0.5 * values * values) * (1.0 / math.sqrt(2.0 * math.pi))
    return normal_cdf + values * density


def shift_ahead(values, offset):
    return jnp.concatenate(
        [values[:, offset:], jnp.zeros((values.shape[0], offset), values.dtype)], axis=1
    )


def stack_taps(flow, spacing):
    return jnp.concatenate([flow] + [shift_ahead(flow, tap * spacing) for tap in (1, 2)], axis=0)


def block_sums(weights_ref, out_ref, wide_ref, sums_ref, in_sem, out_sem, make_flows, spacing):
    shards, trials, block, _ = out_ref.shape
    loads = [
        pltpu.make_async_copy(
            weights_ref.at[:, pl.ds(s * block, block), :], wide_ref.at[s], in_sem.at[s]
        )
        for s in range(shards)
    ]
    stores = [
        pltpu.make_async_copy(sums_ref.at[s], out_ref.at[s], out_sem.at[s]) for s in range(shards)
    ]
    for load in loads:
        load.start()
    stacked = [stack_taps(flow, spacing) for flow in make_flows()]
    for s in range(shards):
        loads[s].wait()
        wide = jnp.concatenate([wide_ref[s, tap] for tap in range(3)], axis=1)
        for trial in range(trials):
            total = jnp.dot(wide, stacked[trial], preferred_element_type=jnp.float32)
            sums_ref[s, trial] = total.astype(sums_ref.dtype)
        stores[s].start()
    for store in stores:
        store.wait()


def second_section(grad_ref, preact_ref, weights_ref, out_ref, *scratch):
    def make_flows():
        return [
            (grad_ref[trial].astype(jnp.float32) * gelu_slope(preact_ref[trial])).astype(jnp.bfloat16)
            for trial in range(grad_ref.shape[0])
        ]

    block_sums(weights_ref, out_ref, *scratch, make_flows, SECOND_DILATION)


def first_section(arrived_ref, grad_ref, preact_ref, weights_ref, out_ref, upper_ref, *scratch):
    def make_flows():
        flows = []
        for trial in range(grad_ref.shape[0]):
            back = arrived_ref[0, trial].astype(jnp.float32)
            for shard in range(1, arrived_ref.shape[0]):
                back = back + arrived_ref[shard, trial].astype(jnp.float32)
            upper = (grad_ref[trial].astype(jnp.float32) + back).astype(jnp.bfloat16)
            upper_ref[trial] = upper
            flows.append((upper.astype(jnp.float32) * preact_ref[trial]).astype(jnp.bfloat16))
        return flows

    block_sums(weights_ref, out_ref, *scratch, make_flows, FIRST_DILATION)


def body(
    spike_rates,
    first_preactivation,
    second_preactivation,
    output_gradient,
    first_kernel,
    second_kernel,
    session_of,
):
    sections, shards = lax.axis_size("section"), lax.axis_size("trial")
    neurons, trials, steps = spike_rates.shape
    own = output_gradient.shape[0]
    channels = first_kernel.shape[1]
    block = neurons // shards
    rows = block * own // 128

    near = pl.BlockSpec(memory_space=pltpu.VMEM)
    far = pl.BlockSpec(memory_space=pltpu.HBM)
    sums_shape = pltpu.HBM((sections, trials, own, steps), jnp.bfloat16)
    upper_shape = jax.ShapeDtypeStruct((trials, own, steps), jnp.bfloat16)
    scratch = [
        pltpu.VMEM((sections, 3, own, own), jnp.bfloat16),
        pltpu.VMEM((sections, trials, own, steps), jnp.bfloat16),
        pltpu.SemaphoreType.DMA((sections,)),
        pltpu.SemaphoreType.DMA((sections,)),
    ]
    params = pltpu.CompilerParams(vmem_limit_bytes=24 * 2**20)
    cost = pl.CostEstimate(
        flops=6 * channels * own * trials * steps,
        bytes_accessed=2 * (3 * channels * own + channels * trials * steps),
        transcendentals=2 * own * trials * steps,
    )

    def exchange(partial):
        return lax.all_to_all(partial, "section", split_axis=0, concat_axis=0, tiled=True)

    grad, first, second = (
        values.transpose(1, 0, 2)
        for values in (output_gradient, first_preactivation, second_preactivation)
    )
    partial = pl.pallas_call(
        second_section,
        in_specs=[near, near, far],
        out_specs=far,
        out_shape=sums_shape,
        scratch_shapes=scratch,
        compiler_params=params,
        cost_estimate=cost,
        name="second_section",
    )(grad, second, pltpu.with_memory_space_constraint(second_kernel, pltpu.HBM))
    place = lax.broadcasted_iota(jnp.int32, (shards, trials), 0)
    ids = jnp.where(place == lax.axis_index("trial"), session_of[None, :], 0).reshape(-1, 128)
    span, layer = shards // 4, 8
    layers = [[start + j for j in range(layer)] for start in range(0, shards, layer)]
    columns = [
        [start + side + j for j in range(0, span, layer)]
        for start in range(0, shards, span)
        for side in range(layer)
    ]
    ids = lax.optimization_barrier((ids, partial))[0]
    ids = lax.psum(ids, "trial", axis_index_groups=layers)
    arrived, ids = lax.optimization_barrier((exchange(partial), ids))
    partial, upper = pl.pallas_call(
        first_section,
        in_specs=[near, near, near, far],
        out_specs=[far, near],
        out_shape=[sums_shape, upper_shape],
        scratch_shapes=scratch,
        compiler_params=params,
        cost_estimate=cost,
        name="first_section",
    )(arrived, grad, gelu_slope(first), pltpu.with_memory_space_constraint(first_kernel, pltpu.HBM))
    ids = lax.optimization_barrier((ids, partial))[0]
    ids = lax.psum(ids, "trial", axis_index_groups=columns)
    arrived, ids = lax.optimization_barrier((exchange(partial), ids))
    ids = ids + sum(
        lax.ppermute(ids, "trial", [(j, (j + k * span) % shards) for j in range(shards)])
        for k in (2, 1, 3)
    )
    moved = jnp.sum(arrived.astype(jnp.float32), axis=0)
    input_gradient = (upper.astype(jnp.float32) + moved).astype(jnp.bfloat16)

    parts = jnp.einsum("nit,ict->nic", spike_rates, input_gradient, preferred_element_type=jnp.float32)
    parts = parts.astype(jnp.bfloat16).reshape(shards, block * trials, own)
    arrived = lax.all_to_all(parts, "trial", split_axis=0, concat_axis=0, tiled=True)
    keys = ids.reshape(shards, 1, trials) * block + lax.broadcasted_iota(jnp.int32, (1, block, 1), 1)
    slots = lax.broadcasted_iota(jnp.int32, (shards * block, 1), 0)
    chosen = (keys.reshape(1, -1) == slots).astype(jnp.bfloat16)
    summed = jnp.dot(chosen, arrived.reshape(-1, own), preferred_element_type=jnp.float32)
    return summed.astype(jnp.bfloat16).reshape(shards, block, own)


def solution(mesh):
    in_specs = (
        P(None, "trial", None),
        P("section", "trial", None),
        P("section", "trial", None),
        P("section", "trial", None),
        P(None, None, "section"),
        P(None, None, "section"),
        P("trial"),
    )
    out_specs = P(None, "trial", "section")
    return jax.shard_map(body, mesh=mesh, in_specs=in_specs, out_specs=out_specs, check_vma=False)
```

time: 124 us -> 103 us (0.83)
  the two profiles are of different devices: /device:TPU:33 before, /device:TPU:1 now
where the time goes in v3:
time: 103 us; the launch traced here: 102 us
  starting transfers between devices  57.9 us (56%)
  blocking collectives  20.2 us (20%)
  waiting for transfers between devices  11.5 us (11%)
  Pallas kernels  6.96 us (7%)
  local copies, waits for them, and re-layouts  4.13 us (4%)
    all_to_all x1, starting transfers between devices, body(): lax.all_to_all(parts, 'trial', split_axis=0, concat_axis=0, tiled=True)  27.5 us
    ppermute x3, starting transfers between devices, body(): lax.ppermute(ids, 'trial', [(j, (j + k * span) % shards) for j in range(s...  21.5 us
    psum x1, blocking collectives, body(): ids = lax.psum(ids, 'trial', axis_index_groups=columns)  11.6 us
    ppermute x3, waiting for transfers between devices, body(): lax.ppermute(ids, 'trial', [(j, (j + k * span) % shards) for j in range(s...  10.9 us
    all_to_all x2, starting transfers between devices, exchange(): lax.all_to_all(partial, 'section', split_axis=0, concat_axis=0, tiled=True)  8.95 us
    psum x1, blocking collectives, body(): ids = lax.psum(ids, 'trial', axis_index_groups=layers)  8.53 us
    pallas_call x1, Pallas kernels, body(): pl.pallas_call(second_section, in_specs=[near, near, far], out_specs=far,...  3.49 us
    pallas_call x1, Pallas kernels, body(): pl.pallas_call(first_section, in_specs=[near, near, near, far], out_specs...  3.47 us
  transfers between devices with their start and end apart: 6, of which 3 were waited for; matrix products, arithmetic and copies ran while one was open for 1% of the time, Pallas kernels for 0%

profile of v3, /device:TPU:1, one launch (start us, length us, event | category | flops | bytes accessed | tf_op | source)
XLA Modules:
  0.0 102.1 jit_solution(16763774547694209724)
XLA Ops:
  0.0 1.2 %copy_bitcast_fusion = (bf16[2,256,256]{2,1,0:T(8,128)(2,1)S(1)}, bf16[2,256,256]{2,1,0:T(8,128)(2,1)S(1)}) fusion(bf16[256,2,256]{2,1,0:T(2,128)(2,1)} %param.9, bf16[256,2,256]{2,1,0:T(2,128)(2,1)} %param.10), kind=kLoop, calls=%fused_computation.19 | loop fusion | bytes 1048576 | tf_op jit(solution)/shard_map/transpose | solution.py:118
  1.2 3.5 %second_section.1 = bf16[4,2,256,256]{3,2,1,0:T(8,128)(2,1)} custom-call(bf16[2,256,256]{2,1,0:T(8,128)(2,1)S(1)} %get-tuple-element.22.grad_ref, bf16[2,256,256]{2,1,0:T(8,128)(2,1)S(1)} %get-tuple-element.21.preact_ref, bf16[3,1024,256]{2,1,0:T(8,128)(2,1)} %weights_ref.2), custom_call_target="tpu_custom_call" | custom-call | flops 805306368 | bytes 2621440 | tf_op jit(solution)/shard_map/second_section/pallas_call | solution.py:121
  4.7 5.0 %all-to-all-start = ((bf16[4,2,256,256]{3,2,1,0:T(8,128)(2,1)}), bf16[4,2,256,256]{3,2,1,0:T(8,128)(2,1)S(1)}, u32[]{:S(2)}, u32[]{:S(2)}) async-start(bf16[4,2,256,256]{3,2,1,0:T(8,128)(2,1)} %second_section.1), calls=%async_computation | async-start | bytes 2097152 | tf_op jit(solution)/shard_map/all_to_all | solution.py:115
  9.8 0.1 iota.35
  10.1 8.5 %psum.14 = s32[2,128]{1,0:T(2,128)S(1)} all-reduce(s32[2,128]{1,0:T(2,128)S(1)} %broadcast_select_fusion), channel_id=1, replica_groups={{0,1,2,3,4,5,6,7},{8,9,10,11,12,13,14,15},{16,17,18,19,20,21,22,23},{24..., use_global_device_ids=true, to_apply=%region_0.1 | all-reduce | flops 256 | bytes 2048 | tf_op jit(solution)/shard_map/psum | solution.py:141
  18.6 0.2 fusion.7.preact_ref
  18.8 0.6 all-to-all-done.arrived_ref
  19.4 3.5 %first_section.1 = (bf16[4,2,256,256]{3,2,1,0:T(8,128)(2,1)}, bf16[2,256,256]{2,1,0:T(8,128)(2,1)S(1)}) custom-call(bf16[4,2,256,256]{3,2,1,0:T(8,128)(2,1)S(1)} %all-to-all-done.arrived_ref, bf16[2,256,256]{2,1,0:T(8,128)(2,1)S(1)} %get-tuple-element.22.grad_ref, f32[2,256,256]{2,1,0:T(8,128)S(1)} %fusion.7.preact_ref, bf16[3,1024,256]{2,1,0:T(8,128)(2,1)} %weights_ref.3), custom_call_target="tpu_custom_call" | custom-call | flops 805306368 | bytes 2621440 | tf_op jit(solution)/shard_map/first_section/pallas_call | solution.py:143
  22.9 4.0 %all-to-all-start.1 = ((bf16[4,2,256,256]{3,2,1,0:T(8,128)(2,1)}), bf16[4,2,256,256]{3,2,1,0:T(8,128)(2,1)S(1)}, u32[]{:S(2)}, u32[]{:S(2)}) async-start(bf16[4,2,256,256]{3,2,1,0:T(8,128)(2,1)} %get-tuple-element.15), calls=%async_computation.1 | async-start | bytes 2097152 | tf_op jit(solution)/shard_map/all_to_all | solution.py:115
  26.9 11.6 %psum.15 = s32[2,128]{1,0:T(2,128)S(1)} all-reduce(s32[2,128]{1,0:T(2,128)S(1)} %psum.14), channel_id=1, replica_groups={{0,8,16,24},{1,9,17,25},{2,10,18,26},{3,11,19,27},{4,12,20,28},{5,13,21..., use_global_device_ids=true, to_apply=%region_1.2 | all-reduce | flops 256 | bytes 2048 | tf_op jit(solution)/shard_map/psum | solution.py:154
  38.5 0.1 convert_reduce_fusion
  38.7 0.3 fusion.1
  39.0 0.5 copy.16
  39.5 1.0 reshape.40
  40.4 27.5 %all-to-all-start.2 = ((bf16[128,8,256]{2,1,0:T(8,128)(2,1)}), bf16[128,8,256]{2,1,0:T(8,128)(2,1)S(1)}, u32[]{:S(2)}, u32[]{:S(2)}) async-start(bf16[128,8,256]{2,1,0:T(8,128)(2,1)} %reshape.40), calls=%async_computation.2 | async-start | bytes 1048576 | tf_op jit(solution)/shard_map/all_to_all | solution.py:165
  67.9 7.7 %collective-permute-start.2 = (s32[2,128]{1,0:T(2,128)S(1)}, s32[2,128]{1,0:T(2,128)S(1)}, u32[]{:S(2)}, u32[]{:S(2)}) collective-permute-start(s32[2,128]{1,0:T(2,128)S(1)} %psum.15), channel_id=1, source_target_pairs={{0,96},{1,97},{2,98},{3,99},{4,100},{5,101},{6,102},{7,103},{8,104... | collective-permute-start | bytes 3080 | tf_op jit(solution)/shard_map/ppermute | solution.py:157
  75.7 1.9 %collective-permute-start.1 = (s32[2,128]{1,0:T(2,128)S(1)}, s32[2,128]{1,0:T(2,128)S(1)}, u32[]{:S(2)}, u32[]{:S(2)}) collective-permute-start(s32[2,128]{1,0:T(2,128)S(1)} %psum.15), channel_id=1, source_target_pairs={{0,32},{1,33},{2,34},{3,35},{4,36},{5,37},{6,38},{7,39},{8,40},{9,... | collective-permute-start | bytes 3080 | tf_op jit(solution)/shard_map/ppermute | solution.py:157
  77.6 11.9 %collective-permute-start = (s32[2,128]{1,0:T(2,128)S(1)}, s32[2,128]{1,0:T(2,128)S(1)}, u32[]{:S(2)}, u32[]{:S(2)}) collective-permute-start(s32[2,128]{1,0:T(2,128)S(1)} %psum.15), channel_id=1, source_target_pairs={{0,64},{1,65},{2,66},{3,67},{4,68},{5,69},{6,70},{7,71},{8,72},{9,... | collective-permute-start | bytes 3080 | tf_op jit(solution)/shard_map/ppermute | solution.py:157
  89.4 2.2 %collective-permute-done.2 = s32[2,128]{1,0:T(2,128)S(1)} collective-permute-done((s32[2,128]{1,0:T(2,128)S(1)}, s32[2,128]{1,0:T(2,128)S(1)}, u32[]{:S(2)}, u32[]{:S(2)}) %collective-permute-start.2) | collective-permute-done | bytes 1056 | tf_op jit(solution)/shard_map/ppermute | solution.py:157
  91.6 8.8 %collective-permute-done = s32[2,128]{1,0:T(2,128)S(1)} collective-permute-done((s32[2,128]{1,0:T(2,128)S(1)}, s32[2,128]{1,0:T(2,128)S(1)}, u32[]{:S(2)}, u32[]{:S(2)}) %collective-permute-start) | collective-permute-done | bytes 1056 | tf_op jit(solution)/shard_map/ppermute | solution.py:157
  100.4 0.1 mul.56
  100.6 0.2 add.55
  100.9 0.5 fusion.2
  101.3 0.8 reshape.42
  (16 shorter events, 0.3 us)
Async XLA Ops:
  0.0 38.6 %copy-start = (bf16[512,2,256]{2,1,0:T(2,128)(2,1)S(1)}, bf16[512,2,256]{2,1,0:T(2,128)(2,1)}, u32[]{:S(2)}) copy-start(bf16[512,2,256]{2,1,0:T(2,128)(2,1)} %param.7) | copy-start | bytes 1572868
  4.7 5.3 %copy-start.2 = (s32[2]{0:T(128)S(1)}, s32[2]{0:T(128)}, u32[]{:S(2)}) copy-start(s32[2]{0:T(128)} %param.13) | copy-start | bytes 28
  4.7 14.0 %copy-start.1 = (bf16[256,2,256]{2,1,0:T(2,128)(2,1)S(1)}, bf16[256,2,256]{2,1,0:T(2,128)(2,1)}, u32[]{:S(2)}) copy-start(bf16[256,2,256]{2,1,0:T(2,128)(2,1)} %param.8) | copy-start | bytes 786436
  4.7 14.7 %all-to-all-start = ((bf16[4,2,256,256]{3,2,1,0:T(8,128)(2,1)}), bf16[4,2,256,256]{3,2,1,0:T(8,128)(2,1)S(1)}, u32[]{:S(2)}, u32[]{:S(2)}) async-start(bf16[4,2,256,256]{3,2,1,0:T(8,128)(2,1)} %second_section.1), calls=%async_computation | async-start | bytes 2097152 | tf_op jit(solution)/shard_map/all_to_all | solution.py:115
  22.9 15.6 %all-to-all-start.1 = ((bf16[4,2,256,256]{3,2,1,0:T(8,128)(2,1)}), bf16[4,2,256,256]{3,2,1,0:T(8,128)(2,1)S(1)}, u32[]{:S(2)}, u32[]{:S(2)}) async-start(bf16[4,2,256,256]{3,2,1,0:T(8,128)(2,1)} %get-tuple-element.15), calls=%async_computation.1 | async-start | bytes 2097152 | tf_op jit(solution)/shard_map/all_to_all | solution.py:115
  40.4 60.4 %all-to-all-start.2 = ((bf16[128,8,256]{2,1,0:T(8,128)(2,1)}), bf16[128,8,256]{2,1,0:T(8,128)(2,1)S(1)}, u32[]{:S(2)}, u32[]{:S(2)}) async-start(bf16[128,8,256]{2,1,0:T(8,128)(2,1)} %reshape.40), calls=%async_computation.2 | async-start | bytes 1048576 | tf_op jit(solution)/shard_map/all_to_all | solution.py:165
  67.9 23.7 %collective-permute-start.2 = (s32[2,128]{1,0:T(2,128)S(1)}, s32[2,128]{1,0:T(2,128)S(1)}, u32[]{:S(2)}, u32[]{:S(2)}) collective-permute-start(s32[2,128]{1,0:T(2,128)S(1)} %psum.15), channel_id=1, source_target_pairs={{0,96},{1,97},{2,98},{3,99},{4,100},{5,101},{6,102},{7,103},{8,104... | collective-permute-start | bytes 3080 | tf_op jit(solution)/shard_map/ppermute | solution.py:157
  75.7 16.0 %collective-permute-start.1 = (s32[2,128]{1,0:T(2,128)S(1)}, s32[2,128]{1,0:T(2,128)S(1)}, u32[]{:S(2)}, u32[]{:S(2)}) collective-permute-start(s32[2,128]{1,0:T(2,128)S(1)} %psum.15), channel_id=1, source_target_pairs={{0,32},{1,33},{2,34},{3,35},{4,36},{5,37},{6,38},{7,39},{8,40},{9,... | collective-permute-start | bytes 3080 | tf_op jit(solution)/shard_map/ppermute | solution.py:157
  77.6 22.8 %collective-permute-start = (s32[2,128]{1,0:T(2,128)S(1)}, s32[2,128]{1,0:T(2,128)S(1)}, u32[]{:S(2)}, u32[]{:S(2)}) collective-permute-start(s32[2,128]{1,0:T(2,128)S(1)} %psum.15), channel_id=1, source_target_pairs={{0,64},{1,65},{2,66},{3,67},{4,68},{5,69},{6,70},{7,71},{8,72},{9,... | collective-permute-start | bytes 3080 | tf_op jit(solution)/shard_map/ppermute | solution.py:157

commit v4 on v3

v4 whole, which is shorter than its diff:
```python
import math

import jax
import jax.numpy as jnp
from jax import lax
from jax.experimental import pallas as pl
from jax.experimental.pallas import tpu as pltpu
from jax.sharding import PartitionSpec as P

FIRST_DILATION = 32
SECOND_DILATION = 64


def gelu_slope(preact):
    values = preact.astype(jnp.float32)
    normal_cdf = 0.5 * (1.0 + lax.erf(values * (1.0 / math.sqrt(2.0))))
    density = jnp.exp(-0.5 * values * values) * (1.0 / math.sqrt(2.0 * math.pi))
    return normal_cdf + values * density


def shift_ahead(values, offset):
    return jnp.concatenate(
        [values[:, offset:], jnp.zeros((values.shape[0], offset), values.dtype)], axis=1
    )


def stack_taps(flow, spacing):
    return jnp.concatenate([flow] + [shift_ahead(flow, tap * spacing) for tap in (1, 2)], axis=0)


def weight_loads(weights_ref, wide_ref, in_sem, first=0):
    count, taps, block, _ = wide_ref.shape
    return [
        pltpu.make_async_copy(
            weights_ref.at[tap, pl.ds((first + s) * block, block), :],
            wide_ref.at[s, tap],
            in_sem.at[s, tap],
        )
        for s in range(count)
        for tap in range(taps)
    ]


def fetch(weights_ref, after_ref, wide_ref, in_sem):
    loads = weight_loads(weights_ref, wide_ref, in_sem)
    for load in loads:
        load.start()
    for load in loads:
        load.wait()


def take_weights(early_ref, wide_ref, loads, s, block):
    if wide_ref is None:
        return [early_ref[tap, s * block : (s + 1) * block, :] for tap in range(early_ref.shape[0])]
    early, taps = early_ref.shape[:2]
    if s < early:
        return [early_ref[s, tap] for tap in range(taps)]
    for load in loads[taps * (s - early) : taps * (s - early + 1)]:
        load.wait()
    return [wide_ref[s - early, tap] for tap in range(taps)]


def block_sums(early_ref, wide_ref, loads, out_ref, sums_ref, out_sem, flows, spacing):
    shards, trials, block, _ = out_ref.shape
    stores = [
        pltpu.make_async_copy(sums_ref.at[s], out_ref.at[s], out_sem.at[s]) for s in range(shards)
    ]
    stacked = [stack_taps(flow, spacing) for flow in flows]
    for s in range(shards):
        wide = jnp.concatenate(take_weights(early_ref, wide_ref, loads, s, block), axis=1)
        for trial in range(trials):
            total = jnp.dot(wide, stacked[trial], preferred_element_type=jnp.float32)
            sums_ref[s, trial] = total.astype(sums_ref.dtype)
        stores[s].start()
    for store in stores:
        store.wait()


def second_section(grad_ref, preact_ref, weights_ref, out_ref, sums_ref, out_sem):
    flows = [
        (grad_ref[trial].astype(jnp.float32) * gelu_slope(preact_ref[trial])).astype(jnp.bfloat16)
        for trial in range(grad_ref.shape[0])
    ]
    block_sums(weights_ref, None, [], out_ref, sums_ref, out_sem, flows, SECOND_DILATION)


def first_section(
    arrived_ref, grad_ref, slope_ref, early_ref, weights_ref, out_ref, upper_ref, sums_ref, out_sem, wide_ref, in_sem
):
    loads = weight_loads(weights_ref, wide_ref, in_sem, first=early_ref.shape[0])
    for load in loads:
        load.start()
    flows = []
    for trial in range(grad_ref.shape[0]):
        back = arrived_ref[0, trial].astype(jnp.float32)
        for shard in range(1, arrived_ref.shape[0]):
            back = back + arrived_ref[shard, trial].astype(jnp.float32)
        upper = (grad_ref[trial].astype(jnp.float32) + back).astype(jnp.bfloat16)
        upper_ref[trial] = upper
        flows.append((upper.astype(jnp.float32) * slope_ref[trial]).astype(jnp.bfloat16))
    block_sums(early_ref, wide_ref, loads, out_ref, sums_ref, out_sem, flows, FIRST_DILATION)


def readin(arrived_ref, upper_ref, spikes_ref, out_ref, parts_ref, out_sem):
    shards, trials, own, _ = arrived_ref.shape
    gradients = []
    for trial in range(trials):
        total = upper_ref[trial].astype(jnp.float32)
        for shard in range(shards):
            total = total + arrived_ref[shard, trial].astype(jnp.float32)
        gradients.append(total.astype(jnp.bfloat16))
    joined = jnp.concatenate(gradients, axis=0)
    chunks, rows, _ = parts_ref.shape
    trial_of_row = lax.rem(lax.broadcasted_iota(jnp.int32, (rows, own), 0), trials)
    stores = []
    for k in range(chunks):
        products = lax.dot_general(
            spikes_ref[k * rows : (k + 1) * rows, :],
            joined,
            (((1,), (1,)), ((), ())),
            preferred_element_type=jnp.float32,
        )
        picked = products[:, :own]
        for trial in range(1, trials):
            picked = jnp.where(
                trial_of_row == trial, products[:, trial * own : (trial + 1) * own], picked
            )
        parts_ref[k] = picked.astype(parts_ref.dtype)
        stores.append(
            pltpu.make_async_copy(
                parts_ref.at[k], out_ref.at[pl.ds(k * rows, rows), :], out_sem.at[k]
            )
        )
        stores[-1].start()
    for store in stores:
        store.wait()


def body(
    spike_rates,
    first_preactivation,
    second_preactivation,
    output_gradient,
    first_kernel,
    second_kernel,
    session_of,
):
    sections, shards = lax.axis_size("section"), lax.axis_size("trial")
    neurons, trials, steps = spike_rates.shape
    own = output_gradient.shape[0]
    channels = first_kernel.shape[1]
    block = neurons // shards
    rows = block * own // 128

    near = pl.BlockSpec(memory_space=pltpu.VMEM)
    far = pl.BlockSpec(memory_space=pltpu.HBM)
    sums_shape = pltpu.HBM((sections, trials, own, steps), jnp.bfloat16)
    upper_shape = jax.ShapeDtypeStruct((trials, own, steps), jnp.bfloat16)
    wide_shape = (sections, 3, own, own)
    scratch = [
        pltpu.VMEM((sections, trials, own, steps), jnp.bfloat16),
        pltpu.SemaphoreType.DMA((sections,)),
    ]
    params = pltpu.CompilerParams(vmem_limit_bytes=10 * 2**20)
    cost = pl.CostEstimate(
        flops=6 * channels * own * trials * steps,
        bytes_accessed=2 * (3 * channels * own + channels * trials * steps),
        transcendentals=2 * own * trials * steps,
    )

    def exchange(partial):
        return lax.all_to_all(partial, "section", split_axis=0, concat_axis=0, tiled=True)

    grad, first, second = (
        values.transpose(1, 0, 2)
        for values in (output_gradient, first_preactivation, second_preactivation)
    )
    partial = pl.pallas_call(
        second_section,
        in_specs=[near, near, near],
        out_specs=far,
        out_shape=sums_shape,
        scratch_shapes=scratch,
        compiler_params=params,
        cost_estimate=cost,
        name="second_section",
    )(grad, second, second_kernel)
    place = lax.broadcasted_iota(jnp.int32, (shards, trials), 0)
    ids = jnp.where(place == lax.axis_index("trial"), session_of[None, :], 0).reshape(-1, 128)
    span, layer = shards // 4, 8
    layers = [[start + j for j in range(layer)] for start in range(0, shards, layer)]
    columns = [
        [start + side + j for j in range(0, span, layer)]
        for start in range(0, shards, span)
        for side in range(layer)
    ]
    ids = lax.optimization_barrier((ids, partial))[0]
    ids = lax.psum(ids, "trial", axis_index_groups=layers)
    first_weights = pltpu.with_memory_space_constraint(first_kernel, pltpu.HBM)
    early_shape = (1, *wide_shape[1:])
    late_shape = (sections - 1, *wide_shape[1:])
    early = pl.pallas_call(
        fetch,
        in_specs=[far, pl.BlockSpec(memory_space=pl.ANY)],
        out_specs=near,
        out_shape=pltpu.VMEM(early_shape, jnp.bfloat16),
        scratch_shapes=[pltpu.SemaphoreType.DMA(early_shape[:2])],
        compiler_params=params,
        cost_estimate=pl.CostEstimate(
            flops=0, bytes_accessed=2 * first_kernel.size, transcendentals=0
        ),
        name="fetch_first_kernel",
    )(first_weights, ids)
    arrived, ids, early = lax.optimization_barrier((exchange(partial), ids, early))
    partial, upper = pl.pallas_call(
        first_section,
        in_specs=[near, near, near, near, far],
        out_specs=[far, near],
        out_shape=[sums_shape, upper_shape],
        scratch_shapes=scratch
        + [pltpu.VMEM(late_shape, jnp.bfloat16), pltpu.SemaphoreType.DMA(late_shape[:2])],
        compiler_params=params,
        cost_estimate=cost,
        name="first_section",
    )(arrived, grad, gelu_slope(first), early, first_weights)
    ids = lax.optimization_barrier((ids, partial))[0]
    ids = lax.psum(ids, "trial", axis_index_groups=columns)
    arrived, ids = lax.optimization_barrier((exchange(partial), ids))
    ids = ids + sum(
        lax.ppermute(ids, "trial", [(j, (j + k * span) % shards) for j in range(shards)])
        for k in (2, 1, 3)
    )
    flat_shape = (neurons * trials, steps)
    parts = pl.pallas_call(
        readin,
        in_specs=[near, near, near],
        out_specs=far,
        out_shape=pltpu.HBM((neurons * trials, own), jnp.bfloat16),
        scratch_shapes=[
            pltpu.VMEM((sections, neurons * trials // sections, own), jnp.bfloat16),
            pltpu.SemaphoreType.DMA((sections,)),
        ],
        compiler_params=params,
        cost_estimate=pl.CostEstimate(
            flops=2 * neurons * trials * trials * own * steps,
            bytes_accessed=4 * neurons * trials * own,
            transcendentals=0,
        ),
        name="readin",
    )(arrived, upper, spike_rates.reshape(flat_shape))
    parts = parts.reshape(shards, block * trials, own)
    arrived = lax.all_to_all(parts, "trial", split_axis=0, concat_axis=0, tiled=True)
    keys = ids.reshape(shards, 1, trials) * block + lax.broadcasted_iota(jnp.int32, (1, block, 1), 1)
    slots = lax.broadcasted_iota(jnp.int32, (shards * block, 1), 0)
    chosen = (keys.reshape(1, -1) == slots).astype(jnp.bfloat16)
    summed = jnp.dot(chosen, arrived.reshape(-1, own), preferred_element_type=jnp.float32)
    return summed.astype(jnp.bfloat16).reshape(shards, block, own)


def solution(mesh):
    in_specs = (
        P(None, "trial", None),
        P("section", "trial", None),
        P("section", "trial", None),
        P("section", "trial", None),
        P(None, None, "section"),
        P(None, None, "section"),
        P("trial"),
    )
    out_specs = P(None, "trial", "section")
    return jax.shard_map(body, mesh=mesh, in_specs=in_specs, out_specs=out_specs, check_vma=False)
```

time: 103 us -> 101 us (0.981)
  blocking collectives: 20.2 us -> 19.1 us
    unnamed x6 -> x8, local copies, waits for them, and re-layouts: 0.02 us -> 1.42 us
    psum x1, blocking collectives: 11.6 us -> 10.6 us  [body(): ids = lax.psum(ids, 'trial', axis_index_groups=columns)]
    pallas_call x2 -> x4, Pallas kernels: 6.96 us -> 7.34 us  [the longest x1 3.13 us: body(): pl.pallas_call(first_section, in_specs=[near, near, near, near, far], out...]
  transfers between devices with their start and end apart: 6 -> 6, of which waited for: 3 -> 1; matrix products, arithmetic and copies ran while one was open for 1% -> 1% of each run, Pallas kernels for 0% -> 1%
where the time goes in v4:
time: 101 us
  starting transfers between devices  58.4 us (58%)
  blocking collectives  19.1 us (19%)
  waiting for transfers between devices  10.9 us (11%)
  Pallas kernels  7.34 us (7%)
  local copies, waits for them, and re-layouts  4.23 us (4%)
    all_to_all x1, starting transfers between devices, body(): lax.all_to_all(parts, 'trial', split_axis=0, concat_axis=0, tiled=True)  27.2 us
    ppermute x3, starting transfers between devices, body(): lax.ppermute(ids, 'trial', [(j, (j + k * span) % shards) for j in range(s...  21.5 us
    ppermute x3, waiting for transfers between devices, body(): lax.ppermute(ids, 'trial', [(j, (j + k * span) % shards) for j in range(s...  10.8 us
    psum x1, blocking collectives, body(): ids = lax.psum(ids, 'trial', axis_index_groups=columns)  10.6 us
    all_to_all x2, starting transfers between devices, exchange(): lax.all_to_all(partial, 'section', split_axis=0, concat_axis=0, tiled=True)  9.65 us
    psum x1, blocking collectives, body(): ids = lax.psum(ids, 'trial', axis_index_groups=layers)  8.53 us
    pallas_call x1, Pallas kernels, body(): pl.pallas_call(first_section, in_specs=[near, near, near, near, far], out...  3.13 us
  transfers between devices with their start and end apart: 6, of which 1 were waited for; matrix products, arithmetic and copies ran while one was open for 1% of the time, Pallas kernels for 1%

profile of v4, /device:TPU:1, one launch (start us, length us, event | category | flops | bytes accessed | tf_op | source)
XLA Modules:
  0.0 100.9 jit_solution(7955591336742718961)
XLA Ops:
  0.0 1.1 %copy_bitcast_fusion = (bf16[2,256,256]{2,1,0:T(8,128)(2,1)S(1)}, bf16[2,256,256]{2,1,0:T(8,128)(2,1)S(1)}) fusion(bf16[256,2,256]{2,1,0:T(2,128)(2,1)} %param.9, bf16[256,2,256]{2,1,0:T(2,128)(2,1)} %param.10), kind=kLoop, calls=%fused_computation.14 | loop fusion | bytes 1048576 | tf_op jit(solution)/shard_map/transpose | solution.py:175
  1.1 1.4 %copy-done = bf16[3,1024,256]{2,1,0:T(8,128)(2,1)S(1)} copy-done((bf16[3,1024,256]{2,1,0:T(8,128)(2,1)S(1)}, bf16[3,1024,256]{2,1,0:T(8,128)(2,1)}, u32[]{:S(2)}) %copy-start) | copy-done | bytes 1572888
  2.5 1.9 %second_section.1 = bf16[4,2,256,256]{3,2,1,0:T(8,128)(2,1)} custom-call(bf16[2,256,256]{2,1,0:T(8,128)(2,1)S(1)} %get-tuple-element.24.grad_ref, bf16[2,256,256]{2,1,0:T(8,128)(2,1)S(1)} %get-tuple-element.23.preact_ref, bf16[3,1024,256]{2,1,0:T(8,128)(2,1)S(1)} %copy-done), custom_call_target="tpu_custom_call" | custom-call | flops 805306368 | bytes 2621440 | tf_op jit(solution)/shard_map/second_section/pallas_call | solution.py:178
  4.4 5.0 %all-to-all-start = ((bf16[4,2,256,256]{3,2,1,0:T(8,128)(2,1)}), bf16[4,2,256,256]{3,2,1,0:T(8,128)(2,1)S(1)}, u32[]{:S(2)}, u32[]{:S(2)}) async-start(bf16[4,2,256,256]{3,2,1,0:T(8,128)(2,1)} %second_section.1), calls=%async_computation | async-start | bytes 2097152 | tf_op jit(solution)/shard_map/all_to_all | solution.py:172
  9.4 0.1 broadcast_in_dim.18
  9.6 0.1 iota.34
  9.7 0.1 iota.35
  9.8 8.5 %psum.14.after_ref = s32[2,128]{1,0:T(2,128)S(1)} all-reduce(s32[2,128]{1,0:T(2,128)S(1)} %broadcast_select_fusion), channel_id=1, replica_groups={{0,1,2,3,4,5,6,7},{8,9,10,11,12,13,14,15},{16,17,18,19,20,21,22,23},{24..., use_global_device_ids=true, to_apply=%region_0.1 | all-reduce | flops 256 | bytes 2048 | tf_op jit(solution)/shard_map/psum | solution.py:198
  18.4 1.1 %fetch_first_kernel.1.early_ref = bf16[1,3,256,256]{3,2,1,0:T(8,128)(2,1)S(1)} custom-call(bf16[3,1024,256]{2,1,0:T(8,128)(2,1)} %weights_ref.5, s32[2,128]{1,0:T(2,128)S(1)} %psum.14.after_ref), custom_call_target="tpu_custom_call" | custom-call | bytes 1572864 | tf_op jit(solution)/shard_map/fetch_first_kernel/pallas_call | solution.py:202
  19.4 0.2 fusion.6.slope_ref
  19.7 3.1 %first_section.1 = (bf16[4,2,256,256]{3,2,1,0:T(8,128)(2,1)}, bf16[2,256,256]{2,1,0:T(8,128)(2,1)S(1)}) custom-call(bf16[4,2,256,256]{3,2,1,0:T(8,128)(2,1)S(1)} %all-to-all-done.arrived_ref, bf16[2,256,256]{2,1,0:T(8,128)(2,1)S(1)} %get-tuple-element.24.grad_ref, f32[2,256,256]{2,1,0:T(8,128)S(1)} %fusion.6.slope_ref, ...), custom_call_target="tpu_custom_call" | custom-call | flops 805306368 | bytes 2621440 | tf_op jit(solution)/shard_map/first_section/pallas_call | solution.py:215
  22.8 4.7 %all-to-all-start.1 = ((bf16[4,2,256,256]{3,2,1,0:T(8,128)(2,1)}), bf16[4,2,256,256]{3,2,1,0:T(8,128)(2,1)S(1)}, u32[]{:S(2)}, u32[]{:S(2)}) async-start(bf16[4,2,256,256]{3,2,1,0:T(8,128)(2,1)} %get-tuple-element.17), calls=%async_computation.1 | async-start | bytes 2097152 | tf_op jit(solution)/shard_map/all_to_all | solution.py:172
  27.5 0.2 reshape.43.spikes_ref
  27.7 10.6 %psum.15 = s32[2,128]{1,0:T(2,128)S(1)} all-reduce(s32[2,128]{1,0:T(2,128)S(1)} %psum.14.after_ref), channel_id=1, replica_groups={{0,8,16,24},{1,9,17,25},{2,10,18,26},{3,11,19,27},{4,12,20,28},{5,13,21..., use_global_device_ids=true, to_apply=%region_1.2 | all-reduce | flops 256 | bytes 2048 | tf_op jit(solution)/shard_map/psum | solution.py:227
  38.3 1.3 %readin.1 = bf16[1024,256]{1,0:T(8,128)(2,1)} custom-call(bf16[4,2,256,256]{3,2,1,0:T(8,128)(2,1)S(1)} %all-to-all-done.1.arrived_ref, bf16[2,256,256]{2,1,0:T(8,128)(2,1)S(1)} %get-tuple-element.22.upper_ref, bf16[1024,256]{1,0:T(8,128)(2,1)S(1)} %reshape.43.spikes_ref), custom_call_target="tpu_custom_call" | custom-call | flops 268435456 | bytes 1048576 | tf_op jit(solution)/shard_map/readin/pallas_call | solution.py:234
  39.5 27.2 %all-to-all-start.2 = ((bf16[128,8,256]{2,1,0:T(8,128)(2,1)}), bf16[128,8,256]{2,1,0:T(8,128)(2,1)S(1)}, u32[]{:S(2)}, u32[]{:S(2)}) async-start(bf16[128,8,256]{2,1,0:T(8,128)(2,1)} %bitcast.19), calls=%async_computation.2 | async-start | bytes 1048576 | tf_op jit(solution)/shard_map/all_to_all | solution.py:252
  66.8 12.3 %collective-permute-start = (s32[2,128]{1,0:T(2,128)S(1)}, s32[2,128]{1,0:T(2,128)S(1)}, u32[]{:S(2)}, u32[]{:S(2)}) collective-permute-start(s32[2,128]{1,0:T(2,128)S(1)} %psum.15), channel_id=1, source_target_pairs={{0,64},{1,65},{2,66},{3,67},{4,68},{5,69},{6,70},{7,71},{8,72},{9,... | collective-permute-start | bytes 3080 | tf_op jit(solution)/shard_map/ppermute | solution.py:230
  79.1 2.4 %collective-permute-start.1 = (s32[2,128]{1,0:T(2,128)S(1)}, s32[2,128]{1,0:T(2,128)S(1)}, u32[]{:S(2)}, u32[]{:S(2)}) collective-permute-start(s32[2,128]{1,0:T(2,128)S(1)} %psum.15), channel_id=1, source_target_pairs={{0,32},{1,33},{2,34},{3,35},{4,36},{5,37},{6,38},{7,39},{8,40},{9,... | collective-permute-start | bytes 3080 | tf_op jit(solution)/shard_map/ppermute | solution.py:230
  81.5 6.8 %collective-permute-start.2 = (s32[2,128]{1,0:T(2,128)S(1)}, s32[2,128]{1,0:T(2,128)S(1)}, u32[]{:S(2)}, u32[]{:S(2)}) collective-permute-start(s32[2,128]{1,0:T(2,128)S(1)} %psum.15), channel_id=1, source_target_pairs={{0,96},{1,97},{2,98},{3,99},{4,100},{5,101},{6,102},{7,103},{8,104... | collective-permute-start | bytes 3080 | tf_op jit(solution)/shard_map/ppermute | solution.py:230
  88.3 10.8 %collective-permute-done = s32[2,128]{1,0:T(2,128)S(1)} collective-permute-done((s32[2,128]{1,0:T(2,128)S(1)}, s32[2,128]{1,0:T(2,128)S(1)}, u32[]{:S(2)}, u32[]{:S(2)}) %collective-permute-start) | collective-permute-done | bytes 1056 | tf_op jit(solution)/shard_map/ppermute | solution.py:230
  99.2 0.1 mul.56
  99.4 0.2 add.52
  99.6 0.5 fusion.1
  100.1 0.8 reshape.46
  (17 shorter events, 0.1 us)
Async XLA Ops:
  1.1 1.4 %copy-start = (bf16[3,1024,256]{2,1,0:T(8,128)(2,1)S(1)}, bf16[3,1024,256]{2,1,0:T(8,128)(2,1)}, u32[]{:S(2)}) copy-start(bf16[3,1024,256]{2,1,0:T(8,128)(2,1)} %weights_ref.3) | copy-start | bytes 4718596
  4.4 5.0 %copy-start.3 = (s32[2]{0:T(128)S(1)}, s32[2]{0:T(128)}, u32[]{:S(2)}) copy-start(s32[2]{0:T(128)} %param.13) | copy-start | bytes 28
  4.4 15.0 %copy-start.2 = (bf16[256,2,256]{2,1,0:T(2,128)(2,1)S(1)}, bf16[256,2,256]{2,1,0:T(2,128)(2,1)}, u32[]{:S(2)}) copy-start(bf16[256,2,256]{2,1,0:T(2,128)(2,1)} %param.8) | copy-start | bytes 786436
  4.4 15.2 %all-to-all-start = ((bf16[4,2,256,256]{3,2,1,0:T(8,128)(2,1)}), bf16[4,2,256,256]{3,2,1,0:T(8,128)(2,1)S(1)}, u32[]{:S(2)}, u32[]{:S(2)}) async-start(bf16[4,2,256,256]{3,2,1,0:T(8,128)(2,1)} %second_section.1), calls=%async_computation | async-start | bytes 2097152 | tf_op jit(solution)/shard_map/all_to_all | solution.py:172
  22.8 4.7 %copy-start.1 = (bf16[512,2,256]{2,1,0:T(2,128)(2,1)S(1)}, bf16[512,2,256]{2,1,0:T(2,128)(2,1)}, u32[]{:S(2)}) copy-start(bf16[512,2,256]{2,1,0:T(2,128)(2,1)} %param.7) | copy-start | bytes 1572868
  22.8 15.4 %all-to-all-start.1 = ((bf16[4,2,256,256]{3,2,1,0:T(8,128)(2,1)}), bf16[4,2,256,256]{3,2,1,0:T(8,128)(2,1)S(1)}, u32[]{:S(2)}, u32[]{:S(2)}) async-start(bf16[4,2,256,256]{3,2,1,0:T(8,128)(2,1)} %get-tuple-element.17), calls=%async_computation.1 | async-start | bytes 2097152 | tf_op jit(solution)/shard_map/all_to_all | solution.py:172
  39.5 60.1 %all-to-all-start.2 = ((bf16[128,8,256]{2,1,0:T(8,128)(2,1)}), bf16[128,8,256]{2,1,0:T(8,128)(2,1)S(1)}, u32[]{:S(2)}, u32[]{:S(2)}) async-start(bf16[128,8,256]{2,1,0:T(8,128)(2,1)} %bitcast.19), calls=%async_computation.2 | async-start | bytes 1048576 | tf_op jit(solution)/shard_map/all_to_all | solution.py:252
  66.8 32.4 %collective-permute-start = (s32[2,128]{1,0:T(2,128)S(1)}, s32[2,128]{1,0:T(2,128)S(1)}, u32[]{:S(2)}, u32[]{:S(2)}) collective-permute-start(s32[2,128]{1,0:T(2,128)S(1)} %psum.15), channel_id=1, source_target_pairs={{0,64},{1,65},{2,66},{3,67},{4,68},{5,69},{6,70},{7,71},{8,72},{9,... | collective-permute-start | bytes 3080 | tf_op jit(solution)/shard_map/ppermute | solution.py:230
  79.1 20.0 %collective-permute-start.1 = (s32[2,128]{1,0:T(2,128)S(1)}, s32[2,128]{1,0:T(2,128)S(1)}, u32[]{:S(2)}, u32[]{:S(2)}) collective-permute-start(s32[2,128]{1,0:T(2,128)S(1)} %psum.15), channel_id=1, source_target_pairs={{0,32},{1,33},{2,34},{3,35},{4,36},{5,37},{6,38},{7,39},{8,40},{9,... | collective-permute-start | bytes 3080 | tf_op jit(solution)/shard_map/ppermute | solution.py:230
  81.5 17.6 %collective-permute-start.2 = (s32[2,128]{1,0:T(2,128)S(1)}, s32[2,128]{1,0:T(2,128)S(1)}, u32[]{:S(2)}, u32[]{:S(2)}) collective-permute-start(s32[2,128]{1,0:T(2,128)S(1)} %psum.15), channel_id=1, source_target_pairs={{0,96},{1,97},{2,98},{3,99},{4,100},{5,101},{6,102},{7,103},{8,104... | collective-permute-start | bytes 3080 | tf_op jit(solution)/shard_map/ppermute | solution.py:230

commit v5 on v4

--- a/solution.py
+++ b/solution.py
@@ -49,25 +49,14 @@
         load.wait()
 
 
-def take_weights(early_ref, wide_ref, loads, s, block):
-    if wide_ref is None:
-        return [early_ref[tap, s * block : (s + 1) * block, :] for tap in range(early_ref.shape[0])]
-    early, taps = early_ref.shape[:2]
-    if s < early:
-        return [early_ref[s, tap] for tap in range(taps)]
-    for load in loads[taps * (s - early) : taps * (s - early + 1)]:
-        load.wait()
-    return [wide_ref[s - early, tap] for tap in range(taps)]
-
-
-def block_sums(early_ref, wide_ref, loads, out_ref, sums_ref, out_sem, flows, spacing):
-    shards, trials, block, _ = out_ref.shape
+def block_sums(weights_of, out_ref, sums_ref, out_sem, flows, spacing):
+    shards, trials, _, _ = out_ref.shape
     stores = [
         pltpu.make_async_copy(sums_ref.at[s], out_ref.at[s], out_sem.at[s]) for s in range(shards)
     ]
     stacked = [stack_taps(flow, spacing) for flow in flows]
     for s in range(shards):
-        wide = jnp.concatenate(take_weights(early_ref, wide_ref, loads, s, block), axis=1)
+        wide = jnp.concatenate(weights_of(s), axis=1)
         for trial in range(trials):
             total = jnp.dot(wide, stacked[trial], preferred_element_type=jnp.float32)
             sums_ref[s, trial] = total.astype(sums_ref.dtype)
@@ -81,15 +70,17 @@
         (grad_ref[trial].astype(jnp.float32) * gelu_slope(preact_ref[trial])).astype(jnp.bfloat16)
         for trial in range(grad_ref.shape[0])
     ]
-    block_sums(weights_ref, None, [], out_ref, sums_ref, out_sem, flows, SECOND_DILATION)
+    block = out_ref.shape[2]
+
+    def weights_of(s):
+        return [weights_ref[tap, s * block : (s + 1) * block, :] for tap in range(3)]
+
+    block_sums(weights_of, out_ref, sums_ref, out_sem, flows, SECOND_DILATION)
 
 
 def first_section(
-    arrived_ref, grad_ref, slope_ref, early_ref, weights_ref, out_ref, upper_ref, sums_ref, out_sem, wide_ref, in_sem
+    arrived_ref, grad_ref, preact_ref, wide_ref, out_ref, upper_ref, sums_ref, out_sem
 ):
-    loads = weight_loads(weights_ref, wide_ref, in_sem, first=early_ref.shape[0])
-    for load in loads:
-        load.start()
     flows = []
     for trial in range(grad_ref.shape[0]):
         back = arrived_ref[0, trial].astype(jnp.float32)
@@ -97,8 +88,13 @@
             back = back + arrived_ref[shard, trial].astype(jnp.float32)
         upper = (grad_ref[trial].astype(jnp.float32) + back).astype(jnp.bfloat16)
         upper_ref[trial] = upper
-        flows.append((upper.astype(jnp.float32) * slope_ref[trial]).astype(jnp.bfloat16))
-    block_sums(early_ref, wide_ref, loads, out_ref, sums_ref, out_sem, flows, FIRST_DILATION)
+        slope = gelu_slope(preact_ref[trial])
+        flows.append((upper.astype(jnp.float32) * slope).astype(jnp.bfloat16))
+
+    def weights_of(s):
+        return [wide_ref[s, tap] for tap in range(3)]
+
+    block_sums(weights_of, out_ref, sums_ref, out_sem, flows, FIRST_DILATION)
 
 
 def readin(arrived_ref, upper_ref, spikes_ref, out_ref, parts_ref, out_sem):
@@ -194,17 +190,16 @@
         for start in range(0, shards, span)
         for side in range(layer)
     ]
+    quarters = [[start + j for j in range(0, shards, span)] for start in range(span)]
     ids = lax.optimization_barrier((ids, partial))[0]
-    ids = lax.psum(ids, "trial", axis_index_groups=layers)
+    ids = lax.psum(ids, "trial", axis_index_groups=columns)
     first_weights = pltpu.with_memory_space_constraint(first_kernel, pltpu.HBM)
-    early_shape = (1, *wide_shape[1:])
-    late_shape = (sections - 1, *wide_shape[1:])
     early = pl.pallas_call(
         fetch,
         in_specs=[far, pl.BlockSpec(memory_space=pl.ANY)],
         out_specs=near,
-        out_shape=pltpu.VMEM(early_shape, jnp.bfloat16),
-        scratch_shapes=[pltpu.SemaphoreType.DMA(early_shape[:2])],
+        out_shape=pltpu.VMEM(wide_shape, jnp.bfloat16),
+        scratch_shapes=[pltpu.SemaphoreType.DMA(wide_shape[:2])],
         compiler_params=params,
         cost_estimate=pl.CostEstimate(
             flops=0, bytes_accessed=2 * first_kernel.size, transcendentals=0
@@ -214,22 +209,17 @@
     arrived, ids, early = lax.optimization_barrier((exchange(partial), ids, early))
     partial, upper = pl.pallas_call(
         first_section,
-        in_specs=[near, near, near, near, far],
+        in_specs=[near, near, near, near],
         out_specs=[far, near],
         out_shape=[sums_shape, upper_shape],
-        scratch_shapes=scratch
-        + [pltpu.VMEM(late_shape, jnp.bfloat16), pltpu.SemaphoreType.DMA(late_shape[:2])],
+        scratch_shapes=scratch,
         compiler_params=params,
         cost_estimate=cost,
         name="first_section",
-    )(arrived, grad, gelu_slope(first), early, first_weights)
+    )(arrived, grad, first, early)
     ids = lax.optimization_barrier((ids, partial))[0]
-    ids = lax.psum(ids, "trial", axis_index_groups=columns)
+    ids = lax.psum(ids, "trial", axis_index_groups=quarters)
     arrived, ids = lax.optimization_barrier((exchange(partial), ids))
-    ids = ids + sum(
-        lax.ppermute(ids, "trial", [(j, (j + k * span) % shards) for j in range(shards)])
-        for k in (2, 1, 3)
-    )
     flat_shape = (neurons * trials, steps)
     parts = pl.pallas_call(
         readin,
@@ -250,6 +240,8 @@
     )(arrived, upper, spike_rates.reshape(flat_shape))
     parts = parts.reshape(shards, block * trials, own)
     arrived = lax.all_to_all(parts, "trial", split_axis=0, concat_axis=0, tiled=True)
+    ids = lax.optimization_barrier((ids, parts))[0]
+    ids = lax.psum(ids, "trial", axis_index_groups=layers)
     keys = ids.reshape(shards, 1, trials) * block + lax.broadcasted_iota(jnp.int32, (1, block, 1), 1)
     slots = lax.broadcasted_iota(jnp.int32, (shards * block, 1), 0)
     chosen = (keys.reshape(1, -1) == slots).astype(jnp.bfloat16)

time: 101 us -> 100 us (0.990)
  the two profiles are of different devices: /device:TPU:1 before, /device:TPU:35 now
where the time goes in v5:
time: 100 us; the launch traced here: 99.6 us
  blocking collectives  36.2 us (36%)
  waiting for transfers between devices  28.6 us (29%)
  starting transfers between devices  23 us (23%)
  Pallas kernels  6.81 us (7%)
  local copies, waits for them, and re-layouts  4.26 us (4%)
    all_to_all x1, waiting for transfers between devices, body(): lax.all_to_all(parts, 'trial', split_axis=0, concat_axis=0, tiled=True)  25.1 us
    psum x1, blocking collectives, body(): ids = lax.psum(ids, 'trial', axis_index_groups=quarters)  20.7 us
    all_to_all x1, starting transfers between devices, body(): lax.all_to_all(parts, 'trial', split_axis=0, concat_axis=0, tiled=True)  13.8 us
    all_to_all x2, starting transfers between devices, exchange(): lax.all_to_all(partial, 'section', split_axis=0, concat_axis=0, tiled=True)  9.21 us
    psum x1, blocking collectives, body(): ids = lax.psum(ids, 'trial', axis_index_groups=layers)  8.04 us
    psum x1, blocking collectives, body(): ids = lax.psum(ids, 'trial', axis_index_groups=columns)  7.44 us
    all_to_all x2, waiting for transfers between devices, exchange(): lax.all_to_all(partial, 'section', split_axis=0, concat_axis=0, tiled=True)  3.55 us
    pallas_call x1, Pallas kernels, body(): pl.pallas_call(first_section, in_specs=[near, near, near, near], out_spec...  2.11 us
  transfers between devices with their start and end apart: 3, of which 2 were waited for; matrix products, arithmetic and copies ran while one was open for 1% of the time, Pallas kernels for 2%

profile of v5, /device:TPU:35, one launch (start us, length us, event | category | flops | bytes accessed | tf_op | source)
XLA Modules:
  0.0 99.6 jit_solution(8239151486995838304)
XLA Ops:
  0.0 1.1 %copy_bitcast_fusion.1 = (bf16[2,256,256]{2,1,0:T(8,128)(2,1)S(1)}, bf16[2,256,256]{2,1,0:T(8,128)(2,1)S(1)}) fusion(bf16[256,2,256]{2,1,0:T(2,128)(2,1)} %param.9, bf16[256,2,256]{2,1,0:T(2,128)(2,1)} %param.10), kind=kLoop, calls=%fused_computation.6 | loop fusion | bytes 1048576 | tf_op jit(solution)/shard_map/transpose | solution.py:171
  1.1 0.0 copy-start
  1.1 1.4 %copy-done = bf16[3,1024,256]{2,1,0:T(8,128)(2,1)S(1)} copy-done((bf16[3,1024,256]{2,1,0:T(8,128)(2,1)S(1)}, bf16[3,1024,256]{2,1,0:T(8,128)(2,1)}, u32[]{:S(2)}) %copy-start) | copy-done | bytes 1572888
  2.5 1.9 %second_section.1 = bf16[4,2,256,256]{3,2,1,0:T(8,128)(2,1)} custom-call(bf16[2,256,256]{2,1,0:T(8,128)(2,1)S(1)} %get-tuple-element.26.grad_ref, bf16[2,256,256]{2,1,0:T(8,128)(2,1)S(1)} %get-tuple-element.25.preact_ref, bf16[3,1024,256]{2,1,0:T(8,128)(2,1)S(1)} %copy-done), custom_call_target="tpu_custom_call" | custom-call | flops 805306368 | bytes 2621440 | tf_op jit(solution)/shard_map/second_section/pallas_call | solution.py:174
  4.4 0.0 copy-start.2
  4.4 4.4 %all-to-all-start = ((bf16[4,2,256,256]{3,2,1,0:T(8,128)(2,1)}), bf16[4,2,256,256]{3,2,1,0:T(8,128)(2,1)S(1)}, u32[]{:S(2)}, u32[]{:S(2)}) async-start(bf16[4,2,256,256]{3,2,1,0:T(8,128)(2,1)} %second_section.1), calls=%async_computation | async-start | bytes 2097152 | tf_op jit(solution)/shard_map/all_to_all | solution.py:168
  8.9 0.1 broadcast_in_dim.18
  9.0 0.1 iota.34
  9.1 0.1 iota.35
  9.3 7.4 %psum.21.after_ref = s32[2,128]{1,0:T(2,128)S(1)} all-reduce(s32[2,128]{1,0:T(2,128)S(1)} %broadcast_select_fusion), channel_id=1, replica_groups={{0,8,16,24},{1,9,17,25},{2,10,18,26},{3,11,19,27},{4,12,20,28},{5,13,21..., use_global_device_ids=true, to_apply=%region_0.1 | all-reduce | flops 256 | bytes 2048 | tf_op jit(solution)/shard_map/psum | solution.py:195
  16.8 1.5 %fetch_first_kernel.1.wide_ref = bf16[4,3,256,256]{3,2,1,0:T(8,128)(2,1)S(1)} custom-call(bf16[3,1024,256]{2,1,0:T(8,128)(2,1)} %weights_ref.3, s32[2,128]{1,0:T(2,128)S(1)} %psum.21.after_ref), custom_call_target="tpu_custom_call" | custom-call | bytes 1572864 | tf_op jit(solution)/shard_map/fetch_first_kernel/pallas_call | solution.py:197
  18.3 3.6 %all-to-all-done.arrived_ref = bf16[4,2,256,256]{3,2,1,0:T(8,128)(2,1)S(1)} async-done(((bf16[4,2,256,256]{3,2,1,0:T(8,128)(2,1)}), bf16[4,2,256,256]{3,2,1,0:T(8,128)(2,1)S(1)}, u32[]{:S(2)}, u32[]{:S(2)}) %all-to-all-start) | async-done | bytes 1048608 | tf_op jit(solution)/shard_map/all_to_all | solution.py:168
  21.9 2.1 %first_section.1 = (bf16[4,2,256,256]{3,2,1,0:T(8,128)(2,1)}, bf16[2,256,256]{2,1,0:T(8,128)(2,1)S(1)}) custom-call(bf16[4,2,256,256]{3,2,1,0:T(8,128)(2,1)S(1)} %all-to-all-done.arrived_ref, bf16[2,256,256]{2,1,0:T(8,128)(2,1)S(1)} %get-tuple-element.26.grad_ref, bf16[2,256,256]{2,1,0:T(8,128)(2,1)S(1)} %bitcast.11, ...), custom_call_target="tpu_custom_call" | custom-call | flops 805306368 | bytes 2621440 | tf_op jit(solution)/shard_map/first_section/pallas_call | solution.py:210
  24.0 4.8 %all-to-all-start.1 = ((bf16[4,2,256,256]{3,2,1,0:T(8,128)(2,1)}), bf16[4,2,256,256]{3,2,1,0:T(8,128)(2,1)S(1)}, u32[]{:S(2)}, u32[]{:S(2)}) async-start(bf16[4,2,256,256]{3,2,1,0:T(8,128)(2,1)} %get-tuple-element.18), calls=%async_computation.1 | async-start | bytes 2097152 | tf_op jit(solution)/shard_map/all_to_all | solution.py:168
  28.8 0.2 reshape.43.spikes_ref
  29.0 20.7 %psum.22 = s32[2,128]{1,0:T(2,128)S(1)} all-reduce(s32[2,128]{1,0:T(2,128)S(1)} %psum.21.after_ref), channel_id=1, replica_groups={{0,32,64,96},{1,33,65,97},{2,34,66,98},{3,35,67,99},{4,36,68,100},{5,37..., use_global_device_ids=true, to_apply=%region_1.2 | all-reduce | flops 256 | bytes 2048 | tf_op jit(solution)/shard_map/psum | solution.py:221
  49.7 1.3 %readin.1 = bf16[1024,256]{1,0:T(8,128)(2,1)} custom-call(bf16[4,2,256,256]{3,2,1,0:T(8,128)(2,1)S(1)} %all-to-all-done.1.arrived_ref, bf16[2,256,256]{2,1,0:T(8,128)(2,1)S(1)} %get-tuple-element.23.upper_ref, bf16[1024,256]{1,0:T(8,128)(2,1)S(1)} %reshape.43.spikes_ref), custom_call_target="tpu_custom_call" | custom-call | flops 268435456 | bytes 1048576 | tf_op jit(solution)/shard_map/readin/pallas_call | solution.py:224
  51.0 13.8 %all-to-all-start.2 = ((bf16[128,8,256]{2,1,0:T(8,128)(2,1)}), bf16[128,8,256]{2,1,0:T(8,128)(2,1)S(1)}, u32[]{:S(2)}, u32[]{:S(2)}) async-start(bf16[128,8,256]{2,1,0:T(8,128)(2,1)} %bitcast.12), calls=%async_computation.2 | async-start | bytes 1048576 | tf_op jit(solution)/shard_map/all_to_all | solution.py:242
  64.8 8.0 %psum.23 = s32[2,128]{1,0:T(2,128)S(1)} all-reduce(s32[2,128]{1,0:T(2,128)S(1)} %psum.22), channel_id=1, replica_groups={{0,1,2,3,4,5,6,7},{8,9,10,11,12,13,14,15},{16,17,18,19,20,21,22,23},{24..., use_global_device_ids=true, to_apply=%region_2.3 | all-reduce | flops 256 | bytes 2048 | tf_op jit(solution)/shard_map/psum | solution.py:244
  72.8 0.1 mul.16
  73.0 0.2 add.30
  73.3 25.1 %all-to-all-done.2 = bf16[128,8,256]{2,1,0:T(8,128)(2,1)S(1)} async-done(((bf16[128,8,256]{2,1,0:T(8,128)(2,1)}), bf16[128,8,256]{2,1,0:T(8,128)(2,1)S(1)}, u32[]{:S(2)}, u32[]{:S(2)}) %all-to-all-start.2) | async-done | bytes 524320 | tf_op jit(solution)/shard_map/all_to_all | solution.py:242
  98.4 0.5 fusion.1
  98.8 0.8 reshape.46
  (12 shorter events, 0.1 us)
Async XLA Ops:
  1.1 1.4 %copy-start = (bf16[3,1024,256]{2,1,0:T(8,128)(2,1)S(1)}, bf16[3,1024,256]{2,1,0:T(8,128)(2,1)}, u32[]{:S(2)}) copy-start(bf16[3,1024,256]{2,1,0:T(8,128)(2,1)} %weights_ref.2) | copy-start | bytes 4718596
  4.4 4.4 %copy-start.3 = (s32[2]{0:T(128)S(1)}, s32[2]{0:T(128)}, u32[]{:S(2)}) copy-start(s32[2]{0:T(128)} %param.13) | copy-start | bytes 28
  4.4 4.8 %copy-start.2 = (bf16[256,2,256]{2,1,0:T(2,128)(2,1)S(1)}, bf16[256,2,256]{2,1,0:T(2,128)(2,1)}, u32[]{:S(2)}) copy-start(bf16[256,2,256]{2,1,0:T(2,128)(2,1)} %param.8) | copy-start | bytes 786436
  4.4 17.4 %all-to-all-start = ((bf16[4,2,256,256]{3,2,1,0:T(8,128)(2,1)}), bf16[4,2,256,256]{3,2,1,0:T(8,128)(2,1)S(1)}, u32[]{:S(2)}, u32[]{:S(2)}) async-start(bf16[4,2,256,256]{3,2,1,0:T(8,128)(2,1)} %second_section.1), calls=%async_computation | async-start | bytes 2097152 | tf_op jit(solution)/shard_map/all_to_all | solution.py:168
  24.0 4.8 %copy-start.1 = (bf16[512,2,256]{2,1,0:T(2,128)(2,1)S(1)}, bf16[512,2,256]{2,1,0:T(2,128)(2,1)}, u32[]{:S(2)}) copy-start(bf16[512,2,256]{2,1,0:T(2,128)(2,1)} %param.7) | copy-start | bytes 1572868
  24.0 25.7 %all-to-all-start.1 = ((bf16[4,2,256,256]{3,2,1,0:T(8,128)(2,1)}), bf16[4,2,256,256]{3,2,1,0:T(8,128)(2,1)S(1)}, u32[]{:S(2)}, u32[]{:S(2)}) async-start(bf16[4,2,256,256]{3,2,1,0:T(8,128)(2,1)} %get-tuple-element.18), calls=%async_computation.1 | async-start | bytes 2097152 | tf_op jit(solution)/shard_map/all_to_all | solution.py:168
  51.0 47.4 %all-to-all-start.2 = ((bf16[128,8,256]{2,1,0:T(8,128)(2,1)}), bf16[128,8,256]{2,1,0:T(8,128)(2,1)S(1)}, u32[]{:S(2)}, u32[]{:S(2)}) async-start(bf16[128,8,256]{2,1,0:T(8,128)(2,1)} %bitcast.12), calls=%async_computation.2 | async-start | bytes 1048576 | tf_op jit(solution)/shard_map/all_to_all | solution.py:242

commit v6 on v5

--- a/solution.py
+++ b/solution.py
@@ -183,16 +183,10 @@
     )(grad, second, second_kernel)
     place = lax.broadcasted_iota(jnp.int32, (shards, trials), 0)
     ids = jnp.where(place == lax.axis_index("trial"), session_of[None, :], 0).reshape(-1, 128)
-    span, layer = shards // 4, 8
-    layers = [[start + j for j in range(layer)] for start in range(0, shards, layer)]
-    columns = [
-        [start + side + j for j in range(0, span, layer)]
-        for start in range(0, shards, span)
-        for side in range(layer)
-    ]
+    span = shards // 4
+    neighbours = [[start + j for j in range(span)] for start in range(0, shards, span)]
     quarters = [[start + j for j in range(0, shards, span)] for start in range(span)]
     ids = lax.optimization_barrier((ids, partial))[0]
-    ids = lax.psum(ids, "trial", axis_index_groups=columns)
     first_weights = pltpu.with_memory_space_constraint(first_kernel, pltpu.HBM)
     early = pl.pallas_call(
         fetch,
@@ -241,7 +235,7 @@
     parts = parts.reshape(shards, block * trials, own)
     arrived = lax.all_to_all(parts, "trial", split_axis=0, concat_axis=0, tiled=True)
     ids = lax.optimization_barrier((ids, parts))[0]
-    ids = lax.psum(ids, "trial", axis_index_groups=layers)
+    ids = lax.psum(ids, "trial", axis_index_groups=neighbours)
     keys = ids.reshape(shards, 1, trials) * block + lax.broadcasted_iota(jnp.int32, (1, block, 1), 1)
     slots = lax.broadcasted_iota(jnp.int32, (shards * block, 1), 0)
     chosen = (keys.reshape(1, -1) == slots).astype(jnp.bfloat16)

time: 100 us -> 100 us (level)
  waiting for transfers between devices: 28.6 us -> 18.5 us
  blocking collectives: 36.2 us -> 46.3 us
    all_to_all x1, waiting for transfers between devices: 25.1 us -> 7.51 us  [body(): lax.all_to_all(parts, 'trial', split_axis=0, concat_axis=0, tiled=True)]
    psum x2 -> x1, blocking collectives: 15.5 us -> 25.6 us  [body(): ids = lax.psum(ids, 'trial', axis_index_groups=neighbours)]
    all_to_all x2, waiting for transfers between devices: 3.55 us -> 11 us  [exchange(): lax.all_to_all(partial, 'section', split_axis=0, concat_axis=0, tiled=True)]
where the time goes in v6:
time: 100 us; the launch traced here: 99.6 us
  blocking collectives  46.3 us (46%)
  starting transfers between devices  23 us (23%)
  waiting for transfers between devices  18.5 us (18%)
  Pallas kernels  6.83 us (7%)
  local copies, waits for them, and re-layouts  4.26 us (4%)
    psum x1, blocking collectives, body(): ids = lax.psum(ids, 'trial', axis_index_groups=neighbours)  25.6 us
    psum x1, blocking collectives, body(): ids = lax.psum(ids, 'trial', axis_index_groups=quarters)  20.7 us
    all_to_all x1, starting transfers between devices, body(): lax.all_to_all(parts, 'trial', split_axis=0, concat_axis=0, tiled=True)  13.8 us
    all_to_all x2, waiting for transfers between devices, exchange(): lax.all_to_all(partial, 'section', split_axis=0, concat_axis=0, tiled=True)  11 us
    all_to_all x2, starting transfers between devices, exchange(): lax.all_to_all(partial, 'section', split_axis=0, concat_axis=0, tiled=True)  9.21 us
    all_to_all x1, waiting for transfers between devices, body(): lax.all_to_all(parts, 'trial', split_axis=0, concat_axis=0, tiled=True)  7.51 us
    pallas_call x1, Pallas kernels, body(): pl.pallas_call(first_section, in_specs=[near, near, near, near], out_spec...  2.11 us
  transfers between devices with their start and end apart: 3, of which 2 were waited for; matrix products, arithmetic and copies ran while one was open for 1% of the time, Pallas kernels for 2%

profile of v6, /device:TPU:35, one launch (start us, length us, event | category | flops | bytes accessed | tf_op | source)
XLA Modules:
  0.0 99.6 jit_solution(14104763516809750045)
XLA Ops:
  0.0 1.1 %copy_bitcast_fusion.1 = (bf16[2,256,256]{2,1,0:T(8,128)(2,1)S(1)}, bf16[2,256,256]{2,1,0:T(8,128)(2,1)S(1)}) fusion(bf16[256,2,256]{2,1,0:T(2,128)(2,1)} %param.9, bf16[256,2,256]{2,1,0:T(2,128)(2,1)} %param.10), kind=kLoop, calls=%fused_computation.6 | loop fusion | bytes 1048576 | tf_op jit(solution)/shard_map/transpose | solution.py:171
  1.1 0.0 copy-start
  1.1 1.4 %copy-done = bf16[3,1024,256]{2,1,0:T(8,128)(2,1)S(1)} copy-done((bf16[3,1024,256]{2,1,0:T(8,128)(2,1)S(1)}, bf16[3,1024,256]{2,1,0:T(8,128)(2,1)}, u32[]{:S(2)}) %copy-start) | copy-done | bytes 1572888
  2.5 1.9 %second_section.1 = bf16[4,2,256,256]{3,2,1,0:T(8,128)(2,1)} custom-call(bf16[2,256,256]{2,1,0:T(8,128)(2,1)S(1)} %get-tuple-element.26.grad_ref, bf16[2,256,256]{2,1,0:T(8,128)(2,1)S(1)} %get-tuple-element.25.preact_ref, bf16[3,1024,256]{2,1,0:T(8,128)(2,1)S(1)} %copy-done), custom_call_target="tpu_custom_call" | custom-call | flops 805306368 | bytes 2621440 | tf_op jit(solution)/shard_map/second_section/pallas_call | solution.py:174
  4.4 0.0 copy-start.3
  4.4 4.4 %all-to-all-start = ((bf16[4,2,256,256]{3,2,1,0:T(8,128)(2,1)}), bf16[4,2,256,256]{3,2,1,0:T(8,128)(2,1)S(1)}, u32[]{:S(2)}, u32[]{:S(2)}) async-start(bf16[4,2,256,256]{3,2,1,0:T(8,128)(2,1)} %second_section.1), calls=%async_computation | async-start | bytes 2097152 | tf_op jit(solution)/shard_map/all_to_all | solution.py:168
  8.9 0.1 broadcast_in_dim.18
  9.0 0.1 iota.34
  9.1 0.1 iota.35
  9.3 1.5 %fetch_first_kernel.1.wide_ref = bf16[4,3,256,256]{3,2,1,0:T(8,128)(2,1)S(1)} custom-call(bf16[3,1024,256]{2,1,0:T(8,128)(2,1)} %weights_ref.3, s32[2,128]{1,0:T(2,128)S(1)} %broadcast_select_fusion.after_ref), custom_call_target="tpu_custom_call" | custom-call | bytes 1572864 | tf_op jit(solution)/shard_map/fetch_first_kernel/pallas_call | solution.py:191
  10.9 11.0 %all-to-all-done.arrived_ref = bf16[4,2,256,256]{3,2,1,0:T(8,128)(2,1)S(1)} async-done(((bf16[4,2,256,256]{3,2,1,0:T(8,128)(2,1)}), bf16[4,2,256,256]{3,2,1,0:T(8,128)(2,1)S(1)}, u32[]{:S(2)}, u32[]{:S(2)}) %all-to-all-start) | async-done | bytes 1048608 | tf_op jit(solution)/shard_map/all_to_all | solution.py:168
  21.9 2.1 %first_section.1 = (bf16[4,2,256,256]{3,2,1,0:T(8,128)(2,1)}, bf16[2,256,256]{2,1,0:T(8,128)(2,1)S(1)}) custom-call(bf16[4,2,256,256]{3,2,1,0:T(8,128)(2,1)S(1)} %all-to-all-done.arrived_ref, bf16[2,256,256]{2,1,0:T(8,128)(2,1)S(1)} %get-tuple-element.26.grad_ref, bf16[2,256,256]{2,1,0:T(8,128)(2,1)S(1)} %bitcast.11, ...), custom_call_target="tpu_custom_call" | custom-call | flops 805306368 | bytes 2621440 | tf_op jit(solution)/shard_map/first_section/pallas_call | solution.py:204
  24.0 0.0 copy-start.1
  24.0 4.8 %all-to-all-start.1 = ((bf16[4,2,256,256]{3,2,1,0:T(8,128)(2,1)}), bf16[4,2,256,256]{3,2,1,0:T(8,128)(2,1)S(1)}, u32[]{:S(2)}, u32[]{:S(2)}) async-start(bf16[4,2,256,256]{3,2,1,0:T(8,128)(2,1)} %get-tuple-element.18), calls=%async_computation.1 | async-start | bytes 2097152 | tf_op jit(solution)/shard_map/all_to_all | solution.py:168
  28.8 0.2 reshape.43.spikes_ref
  29.0 20.7 %psum.14 = s32[2,128]{1,0:T(2,128)S(1)} all-reduce(s32[2,128]{1,0:T(2,128)S(1)} %broadcast_select_fusion.after_ref), channel_id=1, replica_groups={{0,32,64,96},{1,33,65,97},{2,34,66,98},{3,35,67,99},{4,36,68,100},{5,37..., use_global_device_ids=true, to_apply=%region_0.1 | all-reduce | flops 256 | bytes 2048 | tf_op jit(solution)/shard_map/psum | solution.py:215
  49.7 1.3 %readin.1 = bf16[1024,256]{1,0:T(8,128)(2,1)} custom-call(bf16[4,2,256,256]{3,2,1,0:T(8,128)(2,1)S(1)} %all-to-all-done.1.arrived_ref, bf16[2,256,256]{2,1,0:T(8,128)(2,1)S(1)} %get-tuple-element.23.upper_ref, bf16[1024,256]{1,0:T(8,128)(2,1)S(1)} %reshape.43.spikes_ref), custom_call_target="tpu_custom_call" | custom-call | flops 268435456 | bytes 1048576 | tf_op jit(solution)/shard_map/readin/pallas_call | solution.py:218
  51.0 13.8 %all-to-all-start.2 = ((bf16[128,8,256]{2,1,0:T(8,128)(2,1)}), bf16[128,8,256]{2,1,0:T(8,128)(2,1)S(1)}, u32[]{:S(2)}, u32[]{:S(2)}) async-start(bf16[128,8,256]{2,1,0:T(8,128)(2,1)} %bitcast.12), calls=%async_computation.2 | async-start | bytes 1048576 | tf_op jit(solution)/shard_map/all_to_all | solution.py:236
  64.8 25.6 %psum.15 = s32[2,128]{1,0:T(2,128)S(1)} all-reduce(s32[2,128]{1,0:T(2,128)S(1)} %psum.14), channel_id=1, replica_groups={{0,1,2,3,4,5,6,7,8,9,10,11,12,13,14,15,16,17,18,19,20,21,22,23,24,25,26..., use_global_device_ids=true, to_apply=%region_1.2 | all-reduce | flops 256 | bytes 2048 | tf_op jit(solution)/shard_map/psum | solution.py:238
  90.4 0.1 mul.16
  90.6 0.2 add.28
  90.9 7.5 %all-to-all-done.2 = bf16[128,8,256]{2,1,0:T(8,128)(2,1)S(1)} async-done(((bf16[128,8,256]{2,1,0:T(8,128)(2,1)}), bf16[128,8,256]{2,1,0:T(8,128)(2,1)S(1)}, u32[]{:S(2)}, u32[]{:S(2)}) %all-to-all-start.2) | async-done | bytes 524320 | tf_op jit(solution)/shard_map/all_to_all | solution.py:236
  98.4 0.5 fusion.1
  98.8 0.8 reshape.46
  (11 shorter events, 0.1 us)
Async XLA Ops:
  1.1 1.4 %copy-start = (bf16[3,1024,256]{2,1,0:T(8,128)(2,1)S(1)}, bf16[3,1024,256]{2,1,0:T(8,128)(2,1)}, u32[]{:S(2)}) copy-start(bf16[3,1024,256]{2,1,0:T(8,128)(2,1)} %weights_ref.2) | copy-start | bytes 4718596
  4.4 4.4 %copy-start.3 = (s32[2]{0:T(128)S(1)}, s32[2]{0:T(128)}, u32[]{:S(2)}) copy-start(s32[2]{0:T(128)} %param.13) | copy-start | bytes 28
  4.4 4.8 %copy-start.2 = (bf16[256,2,256]{2,1,0:T(2,128)(2,1)S(1)}, bf16[256,2,256]{2,1,0:T(2,128)(2,1)}, u32[]{:S(2)}) copy-start(bf16[256,2,256]{2,1,0:T(2,128)(2,1)} %param.8) | copy-start | bytes 786436
  4.4 17.4 %all-to-all-start = ((bf16[4,2,256,256]{3,2,1,0:T(8,128)(2,1)}), bf16[4,2,256,256]{3,2,1,0:T(8,128)(2,1)S(1)}, u32[]{:S(2)}, u32[]{:S(2)}) async-start(bf16[4,2,256,256]{3,2,1,0:T(8,128)(2,1)} %second_section.1), calls=%async_computation | async-start | bytes 2097152 | tf_op jit(solution)/shard_map/all_to_all | solution.py:168
  24.0 4.8 %copy-start.1 = (bf16[512,2,256]{2,1,0:T(2,128)(2,1)S(1)}, bf16[512,2,256]{2,1,0:T(2,128)(2,1)}, u32[]{:S(2)}) copy-start(bf16[512,2,256]{2,1,0:T(2,128)(2,1)} %param.7) | copy-start | bytes 1572868
  24.0 25.7 %all-to-all-start.1 = ((bf16[4,2,256,256]{3,2,1,0:T(8,128)(2,1)}), bf16[4,2,256,256]{3,2,1,0:T(8,128)(2,1)S(1)}, u32[]{:S(2)}, u32[]{:S(2)}) async-start(bf16[4,2,256,256]{3,2,1,0:T(8,128)(2,1)} %get-tuple-element.18), calls=%async_computation.1 | async-start | bytes 2097152 | tf_op jit(solution)/shard_map/all_to_all | solution.py:168
  51.0 47.4 %all-to-all-start.2 = ((bf16[128,8,256]{2,1,0:T(8,128)(2,1)}), bf16[128,8,256]{2,1,0:T(8,128)(2,1)S(1)}, u32[]{:S(2)}, u32[]{:S(2)}) async-start(bf16[128,8,256]{2,1,0:T(8,128)(2,1)} %bitcast.12), calls=%async_computation.2 | async-start | bytes 1048576 | tf_op jit(solution)/shard_map/all_to_all | solution.py:236
